TPU v7x, 128 devices: a whole 4x4x4 slice. The times are simulated.
128 devices in a mesh: ctx: 32 (over y, z_lo, x), page: 4 (over z_hi, core).
Axes of the slice: x: 4, y: 4, z: 4 (z_hi: 2, z_lo: 2; z = z_hi * 2 + z_lo), core: 2. Of those that a mesh axis runs over, the one named last changes fastest.
Arguments:
- queries: bfloat16 [8192, 8192], P('ctx', 'page'), may hold values from -200 to 200
- keys: bfloat16 [8192, 512], P('ctx', 'page'), may hold values from -6 to 6
- values: bfloat16 [8192, 512], P('ctx', 'page'), may hold values from -6 to 6
- span_table: int32 [64], replicated, may hold values from 0 to 63, each once
- page_slots: int32 [64], replicated, may hold values from 0 to 63, each once
Outputs:
- attended: bfloat16 [8192, 8192], P('ctx', 'page')
- cache_pages: bfloat16 [64, 4, 2, 128, 128], P('ctx')
- cache_scales: float32 [64, 4, 2], P('ctx')
Inputs may be any that keep to these rules, and one draw needn't show every extreme that they name: Stored span i (rows i * 128 to (i + 1) * 128 - 1) holds prompt positions span_table[i] * 128 onward; every value appears once. `page_slots`: every slot is named by exactly one page.
All inputs are finite; a program needn't handle non-finite values. Where the computation divides by a largest or mean magnitude, that divisor is 1e-20 or more.
Results may differ from a plain program's by a relative error of at most 0.0055.
Values may be sent and summed in bfloat16 or wider, within the bound.
No kernel may reach another device: no remote copies, remote signals or barrier semaphores. Data moves between devices by JAX's collectives and lax.ppermute only.
A program may use at most 64 MiB of HBM per device.

v0:
```python
import jax
import jax.numpy as jnp
from jax import lax
from jax.experimental import pallas as pl
from jax.experimental.pallas import tpu as pltpu
from jax.sharding import Mesh, PartitionSpec as P

DH = 128
SP = 128
HEADS = 16
ROWS = HEADS * SP
SCALE2 = DH ** (-0.5) * 1.4426950408889634
TILE = 4
LIMIT = 2.0**100
NT = (((1,), (1,)), ((), ()))
MASKS = ((1, 3), (3, 1))
PIECES = 32
ANY = pl.BlockSpec(memory_space=pl.ANY)
VM = pl.BlockSpec(memory_space=pltpu.VMEM)
SM = pl.BlockSpec(memory_space=pltpu.SMEM)


def tables(span_table, page_slots):
    y, zl, x, core = (lax.axis_index(a) for a in ("y", "zl", "x", "core"))
    index = jnp.arange(2 * PIECES, dtype=jnp.int32)
    part, piece = index // PIECES, index % PIECES
    bit = lambda i: (piece >> i) & 1
    low, high = 1 + 2 * part, 3 - 2 * part
    first = (bit(1) * low) ^ (bit(2) * high)
    second = (bit(3) * low) ^ (bit(4) * high)
    dx = jnp.where(core == 0, first, second)
    dy = jnp.where(core == 0, second, first)
    span = ((y ^ dy) * 8 + (zl ^ bit(0)) * 4 + (x ^ dx)) * 2 + part
    here = span[:, None] == jnp.arange(2 * PIECES, dtype=jnp.int32)[None, :]
    pos = jnp.sum(jnp.where(here, span_table[None, :], 0), axis=1)
    slot = jnp.sum(jnp.where(here, page_slots[None, :], 0), axis=1)
    mine = (y * 8 + zl * 4 + x) * 2 + jnp.arange(2, dtype=jnp.int32)
    want = jnp.sum(jnp.where(slot[None, :] == mine[:, None], index[None, :], 0), axis=1)
    return jnp.concatenate([pos, want])


def rows_of(s):
    return pl.ds(s * SP, SP)


def queries_of(q_ref, s, tile):
    rows = pl.ds(pl.multiple_of(s * SP, SP), SP)
    return jnp.concatenate(
        [q_ref[rows, (tile * TILE + h) * DH : (tile * TILE + h + 1) * DH] for h in range(TILE)], 0
    )


def kept(key, value, keep):
    flag = jnp.full((SP, DH), keep.astype(jnp.float32)).astype(jnp.bfloat16)
    return key * flag, jnp.concatenate([value * flag, flag], axis=1)


def blocks_of(table, s, parts, skip=0):
    limit = table[s * PIECES]
    ks, vs = [], []
    for ref, at in parts:
        for i in range(skip, ref.shape[0]):
            key, value = kept(ref[i, 0], ref[i, 1], table[at + i] < limit)
            ks.append(key)
            vs.append(value)
    return ks, vs


def weigh(score, top, count):
    return jnp.exp2(score * SCALE2 - jnp.concatenate([top] * count, axis=1)).astype(jnp.bfloat16)


def tile_rows(tile):
    return slice(tile * TILE * SP, (tile + 1) * TILE * SP)


def first_kernel(table, q_ref, a_ref, b_ref, top_out, acc_out, top_ref, acc, sems):
    def span(s, carry):
        swapped = jnp.full((2, SP, DH), s) > 0
        own = jnp.where(swapped, b_ref[0], a_ref[0])
        other = jnp.where(swapped, a_ref[0], b_ref[0])
        near_first = table[(1 - s) * PIECES] < table[s * PIECES]
        ks, vs = blocks_of(table, s, ((a_ref, 0), (b_ref, PIECES)), 1)
        key, value = kept(other[0], other[1], near_first)
        ones = jnp.ones((SP, DH), jnp.bfloat16)
        kg = jnp.concatenate([own[0], key] + ks, 0)
        vg = jnp.concatenate([jnp.concatenate([own[1], ones], axis=1), value] + vs, 0)
        for tile in range(HEADS // TILE):
            at = tile_rows(tile)
            score = lax.dot_general(
                queries_of(q_ref, s, tile), kg, NT, preferred_element_type=jnp.float32
            )
            row = lax.broadcasted_iota(jnp.int32, (TILE * SP, SP), 0) % SP
            keep = lax.broadcasted_iota(jnp.int32, (TILE * SP, SP), 1) <= row
            diagonal = jnp.where(keep, score[:, :SP] * SCALE2, -1e30)
            top = jnp.broadcast_to(jnp.max(diagonal, axis=1, keepdims=True), (TILE * SP, SP))
            top_ref[s, at, :] = top
            near = jnp.where(keep, jnp.exp2(diagonal - top), 0.0).astype(jnp.bfloat16)
            weight = jnp.concatenate([near, weigh(score[:, SP:], top, len(ks) + 1)], axis=1)
            acc[s, at, :] = jnp.dot(weight, vg, preferred_element_type=jnp.float32)
        for k, (ref, out) in enumerate(((top_ref, top_out), (acc, acc_out))):
            pltpu.make_async_copy(ref.at[s], out.at[s], sems.at[k, s]).start()
        return carry

    lax.fori_loop(0, 2, span, 0)
    for s in range(2):
        for k, (ref, out) in enumerate(((top_ref, top_out), (acc, acc_out))):
            pltpu.make_async_copy(ref.at[s], out.at[s], sems.at[k, s]).wait()


def span_sums(s, table, q_ref, parts, top_ref, store):
    ks, vs = blocks_of(table, s, parts)
    kg, vg = jnp.concatenate(ks, 0), jnp.concatenate(vs, 0)
    for tile in range(HEADS // TILE):
        score = lax.dot_general(
            queries_of(q_ref, s, tile), kg, NT, preferred_element_type=jnp.float32
        )
        weight = weigh(score, top_ref[s, tile_rows(tile), :], len(ks))
        store(tile, jnp.dot(weight, vg, preferred_element_type=jnp.float32))


def next_kernel(firsts, table, q_ref, top_in, *refs):
    *pieces, acc_out, top_ref, acc, sems = refs
    parts = tuple(zip(pieces, firsts))
    for s in range(2):
        pltpu.make_async_copy(top_in.at[s], top_ref.at[s], sems.at[0, s]).start()

    def span(s, carry):
        pltpu.make_async_copy(top_in.at[s], top_ref.at[s], sems.at[0, s]).wait()

        def store(tile, sums):
            acc[s, tile_rows(tile), :] = sums

        span_sums(s, table, q_ref, parts, top_ref, store)
        pltpu.make_async_copy(acc.at[s], acc_out.at[s], sems.at[1, s]).start()
        return carry

    lax.fori_loop(0, 2, span, 0)
    for s in range(2):
        pltpu.make_async_copy(acc.at[s], acc_out.at[s], sems.at[1, s]).wait()


def last_kernel(
    table, q_ref, top_in, acc1_in, acc2_in, acc3_in, b_ref, mine, core, zh, other, sa, sb, ra, rb,
    out, pages, scales,
    top_ref, acc, acc1, acc2, acc3, sems, worst, hold, far_v, far,
):
    ins = ((top_in, top_ref), (acc1_in, acc1), (acc2_in, acc2), (acc3_in, acc3))
    for s in range(2):
        for k, (i, o) in enumerate(ins):
            pltpu.make_async_copy(i.at[s], o.at[s], sems.at[k, s]).start()
    place(mine, core, zh, other, pages, scales)
    worst[...] = jnp.zeros_like(worst)

    def span(s, carry):
        for k, (i, o) in enumerate(ins):
            pltpu.make_async_copy(i.at[s], o.at[s], sems.at[k, s]).wait()

        def store(tile, sums):
            at = tile_rows(tile)
            both = sums + ((acc1[s, at, :] + acc2[s, at, :]) + acc3[s, at, :])
            total = both[:, DH:]
            worst[...] = jnp.where(total < LIMIT, worst[...], 1.0)
            done = (both[:, :DH] / total).astype(jnp.bfloat16)
            for h in range(TILE):
                head = tile * TILE + h
                rows = pl.ds(pl.multiple_of(s * SP, SP), SP)
                out[rows, head * DH : (head + 1) * DH] = done[h * SP : (h + 1) * SP]

        span_sums(s, table, q_ref, ((b_ref, PIECES + PIECES // 2),), top_ref, store)
        return carry

    lax.fori_loop(0, 2, span, 0)

    @pl.when(jnp.max(worst[...]) > 0.0)
    def _():
        half = PIECES // 2
        fetch = [
            pltpu.make_async_copy(ref, far_v.at[pl.ds(k * half, half)], far.at[k])
            for k, ref in enumerate((sa, ra, sb, rb))
        ]
        for copy in fetch:
            copy.start()
        for copy in fetch:
            copy.wait()
        rescaled(table, q_ref, far_v, out, acc, hold)


def rescaled(table, q_ref, held, out, acc, hold):
    for s in range(2):
        limit = table[s * PIECES]
        hold[...] = jnp.full_like(hold, -1e30)
        acc[...] = jnp.zeros_like(acc)

        def block(i, carry, s=s, limit=limit):
            pos = table[i]

            @pl.when(pos <= limit)
            def _():
                key = held[i, 0]
                value = held[i, 1]

                def head(h, c):
                    at = pl.ds(pl.multiple_of(h * SP, SP), SP)
                    q = q_ref[rows_of(s), pl.ds(pl.multiple_of(h * DH, DH), DH)]
                    score = lax.dot_general(q, key, NT, preferred_element_type=jnp.float32)
                    row = lax.broadcasted_iota(jnp.int32, (SP, SP), 0)
                    col = lax.broadcasted_iota(jnp.int32, (SP, SP), 1)
                    keep = (col + pos * SP) <= (row + limit * SP)
                    score = jnp.where(keep, score * SCALE2, -1e30)
                    old = hold[at, :]
                    new = jnp.maximum(old, jnp.max(score, axis=1, keepdims=True))
                    hold[at, :] = new
                    factor = jnp.exp2(old - new)
                    weight = jnp.where(keep, jnp.exp2(score - new), 0.0)
                    acc[at, :DH] = acc[at, :DH] * factor + jnp.dot(
                        weight.astype(jnp.bfloat16), value, preferred_element_type=jnp.float32
                    )
                    acc[at, DH:] = acc[at, DH:] * factor + jnp.sum(weight, axis=1, keepdims=True)
                    return c

                lax.fori_loop(0, HEADS, head, 0)

            return carry

        lax.fori_loop(0, 2 * PIECES, block, 0)
        for h in range(HEADS):
            out[rows_of(s), h * DH : (h + 1) * DH] = (
                acc[rows_of(h), :DH] / acc[rows_of(h), DH:]
            ).astype(jnp.bfloat16)


def pick_kernel(table, sa, ra, sb, rb, pages, sems):
    half = PIECES // 2
    for j in range(2):
        want = table[2 * PIECES + j]
        for k, ref in enumerate((sa, ra, sb, rb)):

            @pl.when((want >= k * half) & (want < (k + 1) * half))
            def _():
                at = jnp.clip(want - k * half, 0, half - 1)
                pltpu.make_async_copy(ref.at[at], pages.at[j], sems.at[j]).start()

    for j in range(2):
        pltpu.make_async_copy(sa.at[0], pages.at[j], sems.at[j]).wait()


def place(mine, core, zh, other, pages, scales):
    me = lax.axis_index("zh") * 2 + lax.axis_index("core")
    lane = lax.broadcasted_iota(jnp.int32, (1, 4), 1)
    for j in range(2):
        for kind in range(2):
            row = jnp.zeros((1, 4), jnp.float32)
            for away, ref in enumerate((mine, core, zh, other)):
                head = me ^ away
                raw = ref[j, kind].astype(jnp.float32)
                high = jnp.max(jnp.abs(raw), axis=0, keepdims=True)
                scale = jnp.max(high, axis=1, keepdims=True) + 1e-06
                row = jnp.where(lane == head, scale, row)
                pages[j, head, kind] = (raw / scale).astype(jnp.bfloat16)
            scales[j, kind : kind + 1, :] = row


def f32(*shape):
    return jax.ShapeDtypeStruct(shape, jnp.float32)


def bf16(*shape):
    return jax.ShapeDtypeStruct(shape, jnp.bfloat16)


def options():
    return {
        "compiler_params": pltpu.CompilerParams(vmem_limit_bytes=56 * 2**20),
        "cost_estimate": pl.CostEstimate(
            flops=4 * 2 * ROWS * 16 * SP * DH * 2,
            transcendentals=2 * ROWS * 16 * SP,
            bytes_accessed=8 * 2**20,
        ),
    }


TOPS = (2, ROWS, DH)
SUMS = (2, ROWS, 2 * DH)


def sums_of(firsts, name, table, queries, top, *pieces):
    return pl.pallas_call(
        lambda *refs: next_kernel(firsts, *refs),
        out_shape=f32(*SUMS),
        in_specs=[SM, VM, ANY] + [VM] * len(pieces),
        out_specs=ANY,
        scratch_shapes=[
            pltpu.VMEM(TOPS, jnp.float32),
            pltpu.VMEM(SUMS, jnp.float32),
            pltpu.SemaphoreType.DMA((2, 2)),
        ],
        name=name,
        **options(),
    )(table, queries, top, *pieces)


def swap(x, along_first, mask):
    pairs = []
    for y in range(4):
        for xx in range(4):
            for core in range(2):
                on_x = (core == 0) == along_first
                there = (y, xx ^ mask) if on_x else (y ^ mask, xx)
                pairs.append(((y * 4 + xx) * 2 + core, (there[0] * 4 + there[1]) * 2 + core))
    return lax.ppermute(x, ("y", "x", "core"), pairs)


def on_device(queries, keys, values, span_table, page_slots):
    own = jnp.stack([keys.reshape(2, SP, DH), values.reshape(2, SP, DH)], axis=1)[:, None]
    both = jnp.concatenate([own, lax.ppermute(own, "zl", [(0, 1), (1, 0)])], axis=1)
    table = tables(span_table, page_slots)
    held = [both[0], both[1]]
    for stage in range(2):
        come = [swap(held[p], True, MASKS[p][stage]) for p in range(2)]
        held = [jnp.concatenate([held[p], come[p]], axis=0) for p in range(2)]
    come = [swap(held[p], False, MASKS[p][0]) for p in range(2)]
    top, acc1 = pl.pallas_call(
        first_kernel,
        out_shape=(f32(*TOPS), f32(*SUMS)),
        in_specs=[SM] + [VM] * 3,
        out_specs=(ANY, ANY),
        scratch_shapes=[
            pltpu.VMEM(TOPS, jnp.float32),
            pltpu.VMEM(SUMS, jnp.float32),
            pltpu.SemaphoreType.DMA((2, 2)),
        ],
        name="attend_first",
        **options(),
    )(table, queries, held[0], held[1])
    more = come
    held = [jnp.concatenate([held[p], come[p]], axis=0) for p in range(2)]
    held[0], held[1], acc1 = lax.optimization_barrier((held[0], held[1], acc1))
    come = [swap(held[p], False, MASKS[p][1]) for p in range(2)]
    acc2 = sums_of((8, 40), "attend_second", table, queries, top, more[0], more[1])
    mine = pl.pallas_call(
        pick_kernel,
        out_shape=bf16(2, 2, SP, DH),
        in_specs=[SM] + [ANY] * 4,
        out_specs=VM,
        scratch_shapes=[pltpu.SemaphoreType.DMA((2,))],
        name="pick_pages",
    )(table, held[0], come[0], held[1], come[1])
    others = [
        lax.ppermute(mine, ("zh", "core"), [(i, i ^ away) for i in range(4)]) for away in (1, 2, 3)
    ]
    acc3 = sums_of((16,), "attend_third", table, queries, top, come[0])
    attended, pages, scales = pl.pallas_call(
        last_kernel,
        out_shape=(bf16(2 * SP, HEADS * DH), bf16(2, 4, 2, SP, DH), f32(2, 2, 4)),
        in_specs=[SM, VM] + [ANY] * 4 + [VM] * 5 + [ANY] * 4,
        out_specs=(VM, VM, VM),
        scratch_shapes=[
            pltpu.VMEM(TOPS, jnp.float32),
            pltpu.VMEM((ROWS, 2 * DH), jnp.float32),
            pltpu.VMEM(SUMS, jnp.float32),
            pltpu.VMEM(SUMS, jnp.float32),
            pltpu.VMEM(SUMS, jnp.float32),
            pltpu.SemaphoreType.DMA((4, 2)),
            pltpu.VMEM((TILE * SP, DH), jnp.float32),
            pltpu.VMEM((ROWS, DH), jnp.float32),
            pltpu.VMEM((2 * PIECES, 2, SP, DH), jnp.bfloat16),
            pltpu.SemaphoreType.DMA((4,)),
        ],
        name="attend_last",
        **options(),
    )(
        table, queries, top, acc1, acc2, acc3, come[1], mine, *others,
        held[0], held[1], come[0], come[1],
    )
    return attended, pages, scales.transpose(0, 2, 1)


def solution(mesh):
    fine = Mesh(mesh.devices.reshape(4, 2, 4, 2, 2), ("y", "zl", "x", "zh", "core"))
    ctx, page = ("y", "zl", "x"), ("zh", "core")
    return jax.shard_map(
        on_device,
        mesh=fine,
        in_specs=(P(ctx, page), P(ctx, page), P(ctx, page), P(), P()),
        out_specs=(P(ctx, page), P(ctx, None, None, None, None), P(ctx, None, None)),
        check_vma=False,
    )
```

profile of v0, /device:TPU:1, one launch (start us, length us, event | category | flops | bytes accessed | tf_op | source)
XLA Modules:
  0.0 96.4 jit_solution(18031783757986761699)
XLA Ops:
  0.6 0.9 maximum_bitcast_fusion
  1.5 2.5 %collective-permute-start = (bf16[2,1,2,128,128]{4,3,2,1,0:T(8,128)(2,1)S(1)}, bf16[2,1,2,128,128]{4,3,2,1,0:T(8,128)(2,1)S(1)}, u32[]{:S(2)}, u32[]{:S(2)}) collective-permute-start(bf16[2,1,2,128,128]{4,3,2,1,0:T(8,128)(2,1)S(1)} %maximum_bitcast_fusion), channel_id=1, source_target_pairs={{0,16},{16,0},{1,17},{17,1},{2,18},{18,2},{3,19},{19,3},{4,20},{20... | collective-permute-start | bytes 393224 | tf_op jit(solution)/shard_map/ppermute | solution.py:316
  4.1 3.2 %collective-permute-done = bf16[2,1,2,128,128]{4,3,2,1,0:T(8,128)(2,1)S(1)} collective-permute-done((bf16[2,1,2,128,128]{4,3,2,1,0:T(8,128)(2,1)S(1)}, bf16[2,1,2,128,128]{4,3,2,1,0:T(8,128)(2,1)S(1)}, u32[]{:S(2)}, u32[]{:S(2)}) %collective-permute-start) | collective-permute-done | bytes 131104 | tf_op jit(solution)/shard_map/ppermute | solution.py:316
  7.3 2.7 %collective-permute-start.3 = (bf16[2,2,128,128]{3,2,1,0:T(8,128)(2,1)S(1)}, bf16[2,2,128,128]{3,2,1,0:T(8,128)(2,1)S(1)}, u32[]{:S(2)}, u32[]{:S(2)}) collective-permute-start(bf16[2,2,128,128]{3,2,1,0:T(8,128)(2,1)S(1)} %get-tuple-element.21), channel_id=1, source_target_pairs={{0,12},{1,97},{4,8},{5,101},{8,4},{9,105},{12,0},{13,109},{32,44},... | collective-permute-start | bytes 393224 | tf_op jit(solution)/shard_map/ppermute | solution.py:311
  10.0 0.8 select_reduce_fusion.1
  10.9 0.1 collective-permute-start.1
  11.0 1.4 %collective-permute-done.3 = bf16[2,2,128,128]{3,2,1,0:T(8,128)(2,1)S(1)} collective-permute-done((bf16[2,2,128,128]{3,2,1,0:T(8,128)(2,1)S(1)}, bf16[2,2,128,128]{3,2,1,0:T(8,128)(2,1)S(1)}, u32[]{:S(2)}, u32[]{:S(2)}) %collective-permute-start.3) | collective-permute-done | bytes 131104 | tf_op jit(solution)/shard_map/ppermute | solution.py:311
  12.4 0.1 collective-permute-start.4
  12.5 2.2 %collective-permute-done.1 = bf16[2,2,128,128]{3,2,1,0:T(8,128)(2,1)S(1)} collective-permute-done((bf16[2,2,128,128]{3,2,1,0:T(8,128)(2,1)S(1)}, bf16[2,2,128,128]{3,2,1,0:T(8,128)(2,1)S(1)}, u32[]{:S(2)}, u32[]{:S(2)}) %collective-permute-start.1) | collective-permute-done | bytes 131104 | tf_op jit(solution)/shard_map/ppermute | solution.py:311
  14.8 0.5 collective-permute-start.2
  15.3 0.2 fusion.3
  15.5 0.6 pad_add_fusion.table.refs_0_
  16.1 1.7 %collective-permute-done.4 = bf16[4,2,128,128]{3,2,1,0:T(8,128)(2,1)S(1)} collective-permute-done((bf16[4,2,128,128]{3,2,1,0:T(8,128)(2,1)S(1)}, bf16[4,2,128,128]{3,2,1,0:T(8,128)(2,1)S(1)}, u32[]{:S(2)}, u32[]{:S(2)}) %collective-permute-start.4) | collective-permute-done | bytes 262176 | tf_op jit(solution)/shard_map/ppermute | solution.py:311
  17.8 2.5 %collective-permute-start.6 = (bf16[8,2,128,128]{3,2,1,0:T(8,128)(2,1)S(1)}, bf16[8,2,128,128]{3,2,1,0:T(8,128)(2,1)S(1)}, u32[]{:S(2)}, u32[]{:S(2)}) collective-permute-start(bf16[8,2,128,128]{3,2,1,0:T(8,128)(2,1)S(1)} %pad_maximum_fusion.3.b_ref), channel_id=1, source_target_pairs={{0,96},{1,13},{4,100},{5,9},{8,104},{9,5},{12,108},{13,1},{32,64},... | collective-permute-start | bytes 1572872 | tf_op jit(solution)/shard_map/ppermute | solution.py:311
  20.3 1.0 %collective-permute-done.2 = bf16[4,2,128,128]{3,2,1,0:T(8,128)(2,1)S(1)} collective-permute-done((bf16[4,2,128,128]{3,2,1,0:T(8,128)(2,1)S(1)}, bf16[4,2,128,128]{3,2,1,0:T(8,128)(2,1)S(1)}, u32[]{:S(2)}, u32[]{:S(2)}) %collective-permute-start.2) | collective-permute-done | bytes 262176 | tf_op jit(solution)/shard_map/ppermute | solution.py:311
  21.4 1.6 %collective-permute-start.5 = (bf16[8,2,128,128]{3,2,1,0:T(8,128)(2,1)S(1)}, bf16[8,2,128,128]{3,2,1,0:T(8,128)(2,1)S(1)}, u32[]{:S(2)}, u32[]{:S(2)}) collective-permute-start(bf16[8,2,128,128]{3,2,1,0:T(8,128)(2,1)S(1)} %pad_maximum_fusion.2.a_ref), channel_id=1, source_target_pairs={{0,32},{1,5},{4,36},{5,1},{8,40},{9,13},{12,44},{13,9},{32,0},{33,... | collective-permute-start | bytes 1572872 | tf_op jit(solution)/shard_map/ppermute | solution.py:311
  23.0 12.4 %attend_first.1 = (f32[2,2048,128]{2,1,0:T(8,128)}, f32[2,2048,256]{2,1,0:T(8,128)}) custom-call(s32[66]{0:T(128)} %pad_add_fusion.table.refs_0_, bf16[256,2048]{1,0:T(8,128)(2,1)} %q_ref.3, bf16[8,2,128,128]{3,2,1,0:T(8,128)(2,1)} %copy-done.4, bf16[8,2,128,128]{3,2,1,0:T(8,128)(2,1)} %copy-done.3), custom_call_target="tpu_custom_call" | custom-call | flops 8589934592 | bytes 8388608 | tf_op jit(solution)/shard_map/attend_first/pallas_call | solution.py:323
  35.4 0.1 pad_maximum_fusion.1.sb
  35.5 0.1 pad_maximum_fusion.sa
  35.7 2.0 %collective-permute-start.7 = (bf16[16,2,128,128]{3,2,1,0:T(8,128)(2,1)S(1)}, bf16[16,2,128,128]{3,2,1,0:T(8,128)(2,1)S(1)}, u32[]{:S(2)}, u32[]{:S(2)}) collective-permute-start(bf16[16,2,128,128]{3,2,1,0:T(8,128)(2,1)S(1)} %pad_maximum_fusion.sa), channel_id=1, source_target_pairs={{0,96},{1,13},{4,100},{5,9},{8,104},{9,5},{12,108},{13,1},{32,64},... | collective-permute-start | bytes 3145736 | tf_op jit(solution)/shard_map/ppermute | solution.py:311
  37.7 0.2 collective-permute-start.8
  37.9 13.4 %attend_second.1.acc2_in = f32[2,2048,256]{2,1,0:T(8,128)} custom-call(s32[66]{0:T(128)} %pad_add_fusion.table.refs_0_, bf16[256,2048]{1,0:T(8,128)(2,1)} %q_ref.3, f32[2,2048,128]{2,1,0:T(8,128)} %get-tuple-element.11.refs_2_.top_in, bf16[8,2,128,128]{3,2,1,0:T(8,128)(2,1)} %copy-done.6, bf16[8,2,128,128]{3,2,1,0:T(8,128)(2,1)} %copy-done.5), custom_call_target="tpu_custom_call" | custom-call | flops 8589934592 | bytes 8388608 | tf_op jit(solution)/shard_map/attend_second/pallas_call | solution.py:288
  51.4 0.4 collective-permute-done.8.rb.b_ref
  51.8 0.6 copy-done.2
  52.4 2.2 %pick_pages.1.mine = bf16[2,2,128,128]{3,2,1,0:T(8,128)(2,1)} custom-call(s32[66]{0:T(128)} %pad_add_fusion.table.refs_0_, bf16[16,2,128,128]{3,2,1,0:T(8,128)(2,1)} %copy-done.1, bf16[16,2,128,128]{3,2,1,0:T(8,128)(2,1)} %copy-done.2, bf16[16,2,128,128]{3,2,1,0:T(8,128)(2,1)} %copy-done, bf16[16,2,128,128]{3,2,1,0:T(8,128)(2,1)} %collective-permute-done.8.rb.b_ref), custom_call_target="tpu_custom_call" | custom-call | tf_op jit(solution)/shard_map/pick_pages/pallas_call | solution.py:341
  54.6 10.7 %collective-permute-start.11 = (bf16[2,2,128,128]{3,2,1,0:T(8,128)(2,1)}, bf16[2,2,128,128]{3,2,1,0:T(8,128)(2,1)S(1)}, u32[]{:S(2)}, u32[]{:S(2)}) collective-permute-start(bf16[2,2,128,128]{3,2,1,0:T(8,128)(2,1)} %pick_pages.1.mine), channel_id=1, source_target_pairs={{0,3},{1,2},{2,1},{3,0},{4,7},{5,6},{6,5},{7,4},{8,11},{9,10},{10,... | collective-permute-start | bytes 393224 | tf_op jit(solution)/shard_map/ppermute | solution.py:350
  65.3 0.5 collective-permute-start.9
  65.7 13.5 %attend_third.1.acc3_in = f32[2,2048,256]{2,1,0:T(8,128)} custom-call(s32[66]{0:T(128)} %pad_add_fusion.table.refs_0_, bf16[256,2048]{1,0:T(8,128)(2,1)} %q_ref.3, f32[2,2048,128]{2,1,0:T(8,128)} %get-tuple-element.11.refs_2_.top_in, bf16[16,2,128,128]{3,2,1,0:T(8,128)(2,1)} %copy-done.2), custom_call_target="tpu_custom_call" | custom-call | flops 8589934592 | bytes 8388608 | tf_op jit(solution)/shard_map/attend_third/pallas_call | solution.py:288
  79.3 0.6 copy-done.7
  79.9 0.1 copy-done.8
  79.9 0.7 copy-done.9
  80.6 15.6 %attend_last.1 = (bf16[256,2048]{1,0:T(8,128)(2,1)}, bf16[2,4,2,128,128]{4,3,2,1,0:T(8,128)(2,1)}, f32[2,2,4]{2,1,0:T(2,128)}) custom-call(s32[66]{0:T(128)} %pad_add_fusion.table.refs_0_, bf16[256,2048]{1,0:T(8,128)(2,1)} %q_ref.3, f32[2,2048,128]{2,1,0:T(8,128)} %get-tuple-element.11.refs_2_.top_in, f32[2,2048,256]{2,1,0:T(8,128)} %get-tuple-element.13.acc1_in, ...), custom_call_target="tpu_custom_call" | custom-call | flops 8589934592 | bytes 8388608 | tf_op jit(solution)/shard_map/attend_last/pallas_call | solution.py:353
  (30 shorter events, 0.3 us)
Async XLA Ops:
  1.5 5.7 %collective-permute-start = (bf16[2,1,2,128,128]{4,3,2,1,0:T(8,128)(2,1)S(1)}, bf16[2,1,2,128,128]{4,3,2,1,0:T(8,128)(2,1)S(1)}, u32[]{:S(2)}, u32[]{:S(2)}) collective-permute-start(bf16[2,1,2,128,128]{4,3,2,1,0:T(8,128)(2,1)S(1)} %maximum_bitcast_fusion), channel_id=1, source_target_pairs={{0,16},{16,0},{1,17},{17,1},{2,18},{18,2},{3,19},{19,3},{4,20},{20... | collective-permute-start | bytes 393224 | tf_op jit(solution)/shard_map/ppermute | solution.py:316
  7.3 5.1 %collective-permute-start.3 = (bf16[2,2,128,128]{3,2,1,0:T(8,128)(2,1)S(1)}, bf16[2,2,128,128]{3,2,1,0:T(8,128)(2,1)S(1)}, u32[]{:S(2)}, u32[]{:S(2)}) collective-permute-start(bf16[2,2,128,128]{3,2,1,0:T(8,128)(2,1)S(1)} %get-tuple-element.21), channel_id=1, source_target_pairs={{0,12},{1,97},{4,8},{5,101},{8,4},{9,105},{12,0},{13,109},{32,44},... | collective-permute-start | bytes 393224 | tf_op jit(solution)/shard_map/ppermute | solution.py:311
  10.9 3.9 %collective-permute-start.1 = (bf16[2,2,128,128]{3,2,1,0:T(8,128)(2,1)S(1)}, bf16[2,2,128,128]{3,2,1,0:T(8,128)(2,1)S(1)}, u32[]{:S(2)}, u32[]{:S(2)}) collective-permute-start(bf16[2,2,128,128]{3,2,1,0:T(8,128)(2,1)S(1)} %get-tuple-element.22), channel_id=1, source_target_pairs={{0,4},{1,33},{4,0},{5,37},{8,12},{9,41},{12,8},{13,45},{32,36},{33... | collective-permute-start | bytes 393224 | tf_op jit(solution)/shard_map/ppermute | solution.py:311
  12.4 5.3 %collective-permute-start.4 = (bf16[4,2,128,128]{3,2,1,0:T(8,128)(2,1)S(1)}, bf16[4,2,128,128]{3,2,1,0:T(8,128)(2,1)S(1)}, u32[]{:S(2)}, u32[]{:S(2)}) collective-permute-start(bf16[4,2,128,128]{3,2,1,0:T(8,128)(2,1)S(1)} %pad_maximum_fusion.5), channel_id=1, source_target_pairs={{0,4},{1,33},{4,0},{5,37},{8,12},{9,41},{12,8},{13,45},{32,36},{33... | collective-permute-start | bytes 786440 | tf_op jit(solution)/shard_map/ppermute | solution.py:311
  14.8 6.5 %collective-permute-start.2 = (bf16[4,2,128,128]{3,2,1,0:T(8,128)(2,1)S(1)}, bf16[4,2,128,128]{3,2,1,0:T(8,128)(2,1)S(1)}, u32[]{:S(2)}, u32[]{:S(2)}) collective-permute-start(bf16[4,2,128,128]{3,2,1,0:T(8,128)(2,1)S(1)} %pad_maximum_fusion.4), channel_id=1, source_target_pairs={{0,12},{1,97},{4,8},{5,101},{8,4},{9,105},{12,0},{13,109},{32,44},... | collective-permute-start | bytes 786440 | tf_op jit(solution)/shard_map/ppermute | solution.py:311
  17.8 5.2 %copy-start.3 = (bf16[8,2,128,128]{3,2,1,0:T(8,128)(2,1)}, bf16[8,2,128,128]{3,2,1,0:T(8,128)(2,1)S(1)}, u32[]{:S(2)}) copy-start(bf16[8,2,128,128]{3,2,1,0:T(8,128)(2,1)S(1)} %pad_maximum_fusion.3.b_ref) | copy-start | bytes 1572868
  17.8 17.6 %collective-permute-start.6 = (bf16[8,2,128,128]{3,2,1,0:T(8,128)(2,1)S(1)}, bf16[8,2,128,128]{3,2,1,0:T(8,128)(2,1)S(1)}, u32[]{:S(2)}, u32[]{:S(2)}) collective-permute-start(bf16[8,2,128,128]{3,2,1,0:T(8,128)(2,1)S(1)} %pad_maximum_fusion.3.b_ref), channel_id=1, source_target_pairs={{0,96},{1,13},{4,100},{5,9},{8,104},{9,5},{12,108},{13,1},{32,64},... | collective-permute-start | bytes 1572872 | tf_op jit(solution)/shard_map/ppermute | solution.py:311
  21.4 1.6 %copy-start.4 = (bf16[8,2,128,128]{3,2,1,0:T(8,128)(2,1)}, bf16[8,2,128,128]{3,2,1,0:T(8,128)(2,1)S(1)}, u32[]{:S(2)}) copy-start(bf16[8,2,128,128]{3,2,1,0:T(8,128)(2,1)S(1)} %pad_maximum_fusion.2.a_ref) | copy-start | bytes 1572868
  21.4 14.1 %collective-permute-start.5 = (bf16[8,2,128,128]{3,2,1,0:T(8,128)(2,1)S(1)}, bf16[8,2,128,128]{3,2,1,0:T(8,128)(2,1)S(1)}, u32[]{:S(2)}, u32[]{:S(2)}) collective-permute-start(bf16[8,2,128,128]{3,2,1,0:T(8,128)(2,1)S(1)} %pad_maximum_fusion.2.a_ref), channel_id=1, source_target_pairs={{0,32},{1,5},{4,36},{5,1},{8,40},{9,13},{12,44},{13,9},{32,0},{33,... | collective-permute-start | bytes 1572872 | tf_op jit(solution)/shard_map/ppermute | solution.py:311
  35.4 2.5 %copy-start.5 = (bf16[8,2,128,128]{3,2,1,0:T(8,128)(2,1)}, bf16[8,2,128,128]{3,2,1,0:T(8,128)(2,1)S(1)}, u32[]{:S(2)}) copy-start(bf16[8,2,128,128]{3,2,1,0:T(8,128)(2,1)S(1)} %collective-permute-done.6.refs_4_) | copy-start | bytes 1572868
  35.5 15.8 %copy-start = (bf16[16,2,128,128]{3,2,1,0:T(8,128)(2,1)}, bf16[16,2,128,128]{3,2,1,0:T(8,128)(2,1)S(1)}, u32[]{:S(2)}) copy-start(bf16[16,2,128,128]{3,2,1,0:T(8,128)(2,1)S(1)} %pad_maximum_fusion.1.sb) | copy-start | bytes 3145732
  35.5 2.4 %copy-start.6 = (bf16[8,2,128,128]{3,2,1,0:T(8,128)(2,1)}, bf16[8,2,128,128]{3,2,1,0:T(8,128)(2,1)S(1)}, u32[]{:S(2)}) copy-start(bf16[8,2,128,128]{3,2,1,0:T(8,128)(2,1)S(1)} %collective-permute-done.5.refs_3_) | copy-start | bytes 1572868
  35.7 15.7 %copy-start.1 = (bf16[16,2,128,128]{3,2,1,0:T(8,128)(2,1)}, bf16[16,2,128,128]{3,2,1,0:T(8,128)(2,1)S(1)}, u32[]{:S(2)}) copy-start(bf16[16,2,128,128]{3,2,1,0:T(8,128)(2,1)S(1)} %pad_maximum_fusion.sa) | copy-start | bytes 3145732
  35.7 15.7 %collective-permute-start.7 = (bf16[16,2,128,128]{3,2,1,0:T(8,128)(2,1)S(1)}, bf16[16,2,128,128]{3,2,1,0:T(8,128)(2,1)S(1)}, u32[]{:S(2)}, u32[]{:S(2)}) collective-permute-start(bf16[16,2,128,128]{3,2,1,0:T(8,128)(2,1)S(1)} %pad_maximum_fusion.sa), channel_id=1, source_target_pairs={{0,96},{1,13},{4,100},{5,9},{8,104},{9,5},{12,108},{13,1},{32,64},... | collective-permute-start | bytes 3145736 | tf_op jit(solution)/shard_map/ppermute | solution.py:311
  37.7 14.1 %collective-permute-start.8 = (bf16[16,2,128,128]{3,2,1,0:T(8,128)(2,1)S(1)}, bf16[16,2,128,128]{3,2,1,0:T(8,128)(2,1)}, u32[]{:S(2)}, u32[]{:S(2)}) collective-permute-start(bf16[16,2,128,128]{3,2,1,0:T(8,128)(2,1)S(1)} %pad_maximum_fusion.1.sb), channel_id=1, source_target_pairs={{0,32},{1,5},{4,36},{5,1},{8,40},{9,13},{12,44},{13,9},{32,0},{33,... | collective-permute-start | bytes 3145736 | tf_op jit(solution)/shard_map/ppermute | solution.py:311
  51.4 1.0 %copy-start.2 = (bf16[16,2,128,128]{3,2,1,0:T(8,128)(2,1)}, bf16[16,2,128,128]{3,2,1,0:T(8,128)(2,1)S(1)}, u32[]{:S(2)}) copy-start(bf16[16,2,128,128]{3,2,1,0:T(8,128)(2,1)S(1)} %collective-permute-done.7.refs_3_.ra) | copy-start | bytes 3145732
  54.6 24.6 %collective-permute-start.11 = (bf16[2,2,128,128]{3,2,1,0:T(8,128)(2,1)}, bf16[2,2,128,128]{3,2,1,0:T(8,128)(2,1)S(1)}, u32[]{:S(2)}, u32[]{:S(2)}) collective-permute-start(bf16[2,2,128,128]{3,2,1,0:T(8,128)(2,1)} %pick_pages.1.mine), channel_id=1, source_target_pairs={{0,3},{1,2},{2,1},{3,0},{4,7},{5,6},{6,5},{7,4},{8,11},{9,10},{10,... | collective-permute-start | bytes 393224 | tf_op jit(solution)/shard_map/ppermute | solution.py:350
  65.3 14.0 %collective-permute-start.10 = (bf16[2,2,128,128]{3,2,1,0:T(8,128)(2,1)}, bf16[2,2,128,128]{3,2,1,0:T(8,128)(2,1)S(1)}, u32[]{:S(2)}, u32[]{:S(2)}) collective-permute-start(bf16[2,2,128,128]{3,2,1,0:T(8,128)(2,1)} %pick_pages.1.mine), channel_id=1, source_target_pairs={{0,2},{1,3},{2,0},{3,1},{4,6},{5,7},{6,4},{7,5},{8,10},{9,11},{10,... | collective-permute-start | bytes 393224 | tf_op jit(solution)/shard_map/ppermute | solution.py:350
  65.3 14.0 %collective-permute-start.9 = (bf16[2,2,128,128]{3,2,1,0:T(8,128)(2,1)}, bf16[2,2,128,128]{3,2,1,0:T(8,128)(2,1)S(1)}, u32[]{:S(2)}, u32[]{:S(2)}) collective-permute-start(bf16[2,2,128,128]{3,2,1,0:T(8,128)(2,1)} %pick_pages.1.mine), channel_id=1, source_target_pairs={{0,1},{1,0},{2,3},{3,2},{4,5},{5,4},{6,7},{7,6},{8,9},{9,8},{10,11... | collective-permute-start | bytes 393224 | tf_op jit(solution)/shard_map/ppermute | solution.py:350
  79.2 0.7 copy-start.7
  79.2 0.7 copy-start.8
  79.9 0.7 copy-start.9
where the time goes:
time: 96.8 us; the launch traced here: 96.4 us
  Pallas kernels  57.1 us (59%)
  starting transfers between devices  23.4 us (24%)
  waiting for transfers between devices  9.89 us (10%)
  other arithmetic  2.94 us (3%)
  local copies, waits for them, and re-layouts  1.97 us (2%)
  between operations  1.06 us (1%)
    pallas_call x2, Pallas kernels, sums_of(): pl.pallas_call(lambda *refs: next_kernel(firsts, *refs), out_shape=f32(*S...  26.9 us
    pallas_call x1, Pallas kernels, on_device(): pl.pallas_call(last_kernel, out_shape=(bf16(2 * SP, HEADS * DH), bf16(2,...  15.6 us
    pallas_call x1, Pallas kernels, on_device(): pl.pallas_call(first_kernel, out_shape=(f32(*TOPS), f32(*SUMS)), in_specs...  12.4 us
    ppermute x3, starting transfers between devices, on_device(): lax.ppermute(mine, ('zh', 'core'), [(i, i ^ away) for i in range(4)])  11.2 us
    ppermute x8, starting transfers between devices, swap(): return lax.ppermute(x, ('y', 'x', 'core'), pairs)  9.71 us
    ppermute x8, waiting for transfers between devices, swap(): return lax.ppermute(x, ('y', 'x', 'core'), pairs)  6.7 us
    ppermute x1, waiting for transfers between devices, on_device(): lax.ppermute(own, 'zl', [(0, 1), (1, 0)])  3.19 us
    ppermute x1, starting transfers between devices, on_device(): lax.ppermute(own, 'zl', [(0, 1), (1, 0)])  2.55 us
  transfers between devices with their start and end apart: 12, of which 6 were waited for; matrix products, arithmetic and copies ran while one was open for 2% of the time, Pallas kernels for 41%

commit v1 on v0

--- a/solution.py
+++ b/solution.py
@@ -119,33 +119,37 @@
         store(tile, jnp.dot(weight, vg, preferred_element_type=jnp.float32))
 
 
-def next_kernel(firsts, table, q_ref, top_in, *refs):
+def next_kernel(firsts, table, q_ref, top_in, acc_in, *refs):
     *pieces, acc_out, top_ref, acc, sems = refs
     parts = tuple(zip(pieces, firsts))
-    for s in range(2):
-        pltpu.make_async_copy(top_in.at[s], top_ref.at[s], sems.at[0, s]).start()
+    ins = ((top_in, top_ref), (acc_in, acc))
+    for s in range(2):
+        for k, (i, o) in enumerate(ins):
+            pltpu.make_async_copy(i.at[s], o.at[s], sems.at[k, s]).start()
 
     def span(s, carry):
-        pltpu.make_async_copy(top_in.at[s], top_ref.at[s], sems.at[0, s]).wait()
+        for k, (i, o) in enumerate(ins):
+            pltpu.make_async_copy(i.at[s], o.at[s], sems.at[k, s]).wait()
 
         def store(tile, sums):
-            acc[s, tile_rows(tile), :] = sums
+            at = tile_rows(tile)
+            acc[s, at, :] = acc[s, at, :] + sums
 
         span_sums(s, table, q_ref, parts, top_ref, store)
-        pltpu.make_async_copy(acc.at[s], acc_out.at[s], sems.at[1, s]).start()
+        pltpu.make_async_copy(acc.at[s], acc_out.at[s], sems.at[2, s]).start()
         return carry
 
     lax.fori_loop(0, 2, span, 0)
     for s in range(2):
-        pltpu.make_async_copy(acc.at[s], acc_out.at[s], sems.at[1, s]).wait()
+        pltpu.make_async_copy(acc.at[s], acc_out.at[s], sems.at[2, s]).wait()
 
 
 def last_kernel(
-    table, q_ref, top_in, acc1_in, acc2_in, acc3_in, b_ref, mine, core, zh, other, sa, sb, ra, rb,
+    table, q_ref, top_in, acc_in, b_ref, mine, core, zh, other, sa, sb, ra, rb,
     out, pages, scales,
-    top_ref, acc, acc1, acc2, acc3, sems, worst, hold, far_v, far,
+    top_ref, acc, hold, sems, worst, far_v, far,
 ):
-    ins = ((top_in, top_ref), (acc1_in, acc1), (acc2_in, acc2), (acc3_in, acc3))
+    ins = ((top_in, top_ref), (acc_in, acc))
     for s in range(2):
         for k, (i, o) in enumerate(ins):
             pltpu.make_async_copy(i.at[s], o.at[s], sems.at[k, s]).start()
@@ -158,7 +162,7 @@
 
         def store(tile, sums):
             at = tile_rows(tile)
-            both = sums + ((acc1[s, at, :] + acc2[s, at, :]) + acc3[s, at, :])
+            both = acc[s, at, :] + sums
             total = both[:, DH:]
             worst[...] = jnp.where(total < LIMIT, worst[...], 1.0)
             done = (both[:, :DH] / total).astype(jnp.bfloat16)
@@ -183,7 +187,7 @@
             copy.start()
         for copy in fetch:
             copy.wait()
-        rescaled(table, q_ref, far_v, out, acc, hold)
+        rescaled(table, q_ref, far_v, out, acc.at[0], hold)
 
 
 def rescaled(table, q_ref, held, out, acc, hold):
@@ -269,12 +273,12 @@
     return jax.ShapeDtypeStruct(shape, jnp.bfloat16)
 
 
-def options():
+def options(spans):
     return {
         "compiler_params": pltpu.CompilerParams(vmem_limit_bytes=56 * 2**20),
         "cost_estimate": pl.CostEstimate(
-            flops=4 * 2 * ROWS * 16 * SP * DH * 2,
-            transcendentals=2 * ROWS * 16 * SP,
+            flops=4 * 2 * ROWS * spans * SP * DH * 2,
+            transcendentals=2 * ROWS * spans * SP,
             bytes_accessed=8 * 2**20,
         ),
     }
@@ -284,20 +288,24 @@
 SUMS = (2, ROWS, 2 * DH)
 
 
-def sums_of(firsts, name, table, queries, top, *pieces):
+def state():
+    return [
+        pltpu.VMEM(TOPS, jnp.float32),
+        pltpu.VMEM(SUMS, jnp.float32),
+        pltpu.SemaphoreType.DMA((3, 2)),
+    ]
+
+
+def sums_of(firsts, name, table, queries, top, acc, *pieces):
     return pl.pallas_call(
         lambda *refs: next_kernel(firsts, *refs),
         out_shape=f32(*SUMS),
-        in_specs=[SM, VM, ANY] + [VM] * len(pieces),
+        in_specs=[SM, VM, ANY, ANY] + [VM] * len(pieces),
         out_specs=ANY,
-        scratch_shapes=[
-            pltpu.VMEM(TOPS, jnp.float32),
-            pltpu.VMEM(SUMS, jnp.float32),
-            pltpu.SemaphoreType.DMA((2, 2)),
-        ],
+        scratch_shapes=state(),
         name=name,
-        **options(),
-    )(table, queries, top, *pieces)
+        **options(sum(p.shape[0] for p in pieces)),
+    )(table, queries, top, acc, *pieces)
 
 
 def swap(x, along_first, mask):
@@ -316,28 +324,33 @@
     both = jnp.concatenate([own, lax.ppermute(own, "zl", [(0, 1), (1, 0)])], axis=1)
     table = tables(span_table, page_slots)
     held = [both[0], both[1]]
-    for stage in range(2):
-        come = [swap(held[p], True, MASKS[p][stage]) for p in range(2)]
-        held = [jnp.concatenate([held[p], come[p]], axis=0) for p in range(2)]
-    come = [swap(held[p], False, MASKS[p][0]) for p in range(2)]
-    top, acc1 = pl.pallas_call(
+
+    def exchange(held, along_first, stage):
+        return [swap(held[p], along_first, MASKS[p][stage]) for p in range(2)]
+
+    def grown(held, come):
+        return [jnp.concatenate([held[p], come[p]], axis=0) for p in range(2)]
+
+    held = grown(held, exchange(held, True, 0))
+    come = exchange(held, True, 1)
+    top, acc = pl.pallas_call(
         first_kernel,
         out_shape=(f32(*TOPS), f32(*SUMS)),
         in_specs=[SM] + [VM] * 3,
         out_specs=(ANY, ANY),
-        scratch_shapes=[
-            pltpu.VMEM(TOPS, jnp.float32),
-            pltpu.VMEM(SUMS, jnp.float32),
-            pltpu.SemaphoreType.DMA((2, 2)),
-        ],
+        scratch_shapes=state(),
         name="attend_first",
-        **options(),
+        **options(8),
     )(table, queries, held[0], held[1])
-    more = come
-    held = [jnp.concatenate([held[p], come[p]], axis=0) for p in range(2)]
-    held[0], held[1], acc1 = lax.optimization_barrier((held[0], held[1], acc1))
-    come = [swap(held[p], False, MASKS[p][1]) for p in range(2)]
-    acc2 = sums_of((8, 40), "attend_second", table, queries, top, more[0], more[1])
+    for stage in range(2):
+        more = come
+        held = grown(held, come)
+        held[0], held[1], acc = lax.optimization_barrier((held[0], held[1], acc))
+        come = exchange(held, False, stage)
+        at = 4 << stage
+        acc = sums_of(
+            (at, PIECES + at), ("attend_second", "attend_third")[stage], table, queries, top, acc, *more
+        )
     mine = pl.pallas_call(
         pick_kernel,
         out_shape=bf16(2, 2, SP, DH),
@@ -349,28 +362,25 @@
     others = [
         lax.ppermute(mine, ("zh", "core"), [(i, i ^ away) for i in range(4)]) for away in (1, 2, 3)
     ]
-    acc3 = sums_of((16,), "attend_third", table, queries, top, come[0])
+    acc = sums_of((16,), "attend_fourth", table, queries, top, acc, come[0])
     attended, pages, scales = pl.pallas_call(
         last_kernel,
         out_shape=(bf16(2 * SP, HEADS * DH), bf16(2, 4, 2, SP, DH), f32(2, 2, 4)),
-        in_specs=[SM, VM] + [ANY] * 4 + [VM] * 5 + [ANY] * 4,
+        in_specs=[SM, VM] + [ANY] * 2 + [VM] * 5 + [ANY] * 4,
         out_specs=(VM, VM, VM),
         scratch_shapes=[
             pltpu.VMEM(TOPS, jnp.float32),
-            pltpu.VMEM((ROWS, 2 * DH), jnp.float32),
             pltpu.VMEM(SUMS, jnp.float32),
-            pltpu.VMEM(SUMS, jnp.float32),
-            pltpu.VMEM(SUMS, jnp.float32),
-            pltpu.SemaphoreType.DMA((4, 2)),
+            pltpu.VMEM((ROWS, DH), jnp.float32),
+            pltpu.SemaphoreType.DMA((2, 2)),
             pltpu.VMEM((TILE * SP, DH), jnp.float32),
-            pltpu.VMEM((ROWS, DH), jnp.float32),
             pltpu.VMEM((2 * PIECES, 2, SP, DH), jnp.bfloat16),
             pltpu.SemaphoreType.DMA((4,)),
         ],
         name="attend_last",
-        **options(),
+        **options(16),
     )(
-        table, queries, top, acc1, acc2, acc3, come[1], mine, *others,
+        table, queries, top, acc, come[1], mine, *others,
         held[0], held[1], come[0], come[1],
     )
     return attended, pages, scales.transpose(0, 2, 1)

time: 96.8 us -> 93.1 us (0.962)
  Pallas kernels: 57.1 us -> 62.3 us
  starting transfers between devices: 23.4 us -> 18.3 us
  waiting for transfers between devices: 9.89 us -> 5.72 us
    pallas_call x2 -> x3, Pallas kernels: 26.9 us -> 37.9 us  [sums_of(): pl.pallas_call(lambda *refs: next_kernel(firsts, *refs), out_shape=f32(*S...]
    pallas_call x1, Pallas kernels: 12.4 us -> 7.9 us  [on_device(): pl.pallas_call(first_kernel, out_shape=(f32(*TOPS), f32(*SUMS)), in_specs...]
    ppermute x8, waiting for transfers between devices: 6.7 us -> 3.4 us  [swap(): return lax.ppermute(x, ('y', 'x', 'core'), pairs)]
    ppermute x3, starting transfers between devices: 11.2 us -> 7.98 us  [on_device(): lax.ppermute(mine, ('zh', 'core'), [(i, i ^ away) for i in range(4)])]
    ppermute x8, starting transfers between devices: 9.71 us -> 7.82 us  [swap(): return lax.ppermute(x, ('y', 'x', 'core'), pairs)]
    pallas_call x1, Pallas kernels: 15.6 us -> 14.3 us  [on_device(): pl.pallas_call(last_kernel, out_shape=(bf16(2 * SP, HEADS * DH), bf16(2,...]
    unnamed x20 -> x24, local copies, waits for them, and re-layouts: 1.97 us -> 2.33 us
  transfers between devices with their start and end apart: 12 -> 12, of which waited for: 6 -> 4; matrix products, arithmetic and copies ran while one was open for 2% -> 2% of each run, Pallas kernels for 41% -> 49%
where the time goes in v1:
time: 93.1 us; the launch traced here: 92.7 us
  Pallas kernels  62.3 us (67%)
  starting transfers between devices  18.3 us (20%)
  waiting for transfers between devices  5.72 us (6%)
  other arithmetic  2.97 us (3%)
  local copies, waits for them, and re-layouts  2.33 us (3%)
  between operations  1.09 us (1%)
    pallas_call x3, Pallas kernels, sums_of(): pl.pallas_call(lambda *refs: next_kernel(firsts, *refs), out_shape=f32(*S...  37.9 us
    pallas_call x1, Pallas kernels, on_device(): pl.pallas_call(last_kernel, out_shape=(bf16(2 * SP, HEADS * DH), bf16(2,...  14.3 us
    ppermute x3, starting transfers between devices, on_device(): lax.ppermute(mine, ('zh', 'core'), [(i, i ^ away) for i in range(4)])  7.98 us
    pallas_call x1, Pallas kernels, on_device(): pl.pallas_call(first_kernel, out_shape=(f32(*TOPS), f32(*SUMS)), in_specs...  7.9 us
    ppermute x8, starting transfers between devices, swap(): return lax.ppermute(x, ('y', 'x', 'core'), pairs)  7.82 us
    ppermute x8, waiting for transfers between devices, swap(): return lax.ppermute(x, ('y', 'x', 'core'), pairs)  3.4 us
    ppermute x1, starting transfers between devices, on_device(): lax.ppermute(own, 'zl', [(0, 1), (1, 0)])  2.55 us
    unnamed x24, local copies, waits for them, and re-layouts  2.33 us
  transfers between devices with their start and end apart: 12, of which 4 were waited for; matrix products, arithmetic and copies ran while one was open for 2% of the time, Pallas kernels for 49%

profile of v1, /device:TPU:1, one launch (start us, length us, event | category | flops | bytes accessed | tf_op | source)
XLA Modules:
  0.0 92.7 jit_solution(12784266274052138260)
XLA Ops:
  0.6 0.9 maximum_bitcast_fusion
  1.5 2.5 %collective-permute-start = (bf16[2,1,2,128,128]{4,3,2,1,0:T(8,128)(2,1)S(1)}, bf16[2,1,2,128,128]{4,3,2,1,0:T(8,128)(2,1)S(1)}, u32[]{:S(2)}, u32[]{:S(2)}) collective-permute-start(bf16[2,1,2,128,128]{4,3,2,1,0:T(8,128)(2,1)S(1)} %maximum_bitcast_fusion), channel_id=1, source_target_pairs={{0,16},{16,0},{1,17},{17,1},{2,18},{18,2},{3,19},{19,3},{4,20},{20... | collective-permute-start | bytes 393224 | tf_op jit(solution)/shard_map/ppermute | solution.py:324
  4.1 0.8 select_reduce_fusion.1
  5.0 2.3 %collective-permute-done = bf16[2,1,2,128,128]{4,3,2,1,0:T(8,128)(2,1)S(1)} collective-permute-done((bf16[2,1,2,128,128]{4,3,2,1,0:T(8,128)(2,1)S(1)}, bf16[2,1,2,128,128]{4,3,2,1,0:T(8,128)(2,1)S(1)}, u32[]{:S(2)}, u32[]{:S(2)}) %collective-permute-start) | collective-permute-done | bytes 131104 | tf_op jit(solution)/shard_map/ppermute | solution.py:324
  7.3 2.7 %collective-permute-start.2 = (bf16[2,2,128,128]{3,2,1,0:T(8,128)(2,1)S(1)}, bf16[2,2,128,128]{3,2,1,0:T(8,128)(2,1)S(1)}, u32[]{:S(2)}, u32[]{:S(2)}) collective-permute-start(bf16[2,2,128,128]{3,2,1,0:T(8,128)(2,1)S(1)} %get-tuple-element.27), channel_id=1, source_target_pairs={{0,12},{1,97},{4,8},{5,101},{8,4},{9,105},{12,0},{13,109},{32,44},... | collective-permute-start | bytes 393224 | tf_op jit(solution)/shard_map/ppermute | solution.py:319
  10.0 0.2 fusion.3
  10.2 0.1 collective-permute-start.1
  10.3 0.7 pad_add_fusion.table.refs_0_
  10.9 1.5 %collective-permute-done.2 = bf16[2,2,128,128]{3,2,1,0:T(8,128)(2,1)S(1)} collective-permute-done((bf16[2,2,128,128]{3,2,1,0:T(8,128)(2,1)S(1)}, bf16[2,2,128,128]{3,2,1,0:T(8,128)(2,1)S(1)}, u32[]{:S(2)}, u32[]{:S(2)}) %collective-permute-start.2) | collective-permute-done | bytes 131104 | tf_op jit(solution)/shard_map/ppermute | solution.py:319
  12.4 0.1 collective-permute-start.4
  12.5 1.8 %collective-permute-done.1 = bf16[2,2,128,128]{3,2,1,0:T(8,128)(2,1)S(1)} collective-permute-done((bf16[2,2,128,128]{3,2,1,0:T(8,128)(2,1)S(1)}, bf16[2,2,128,128]{3,2,1,0:T(8,128)(2,1)S(1)}, u32[]{:S(2)}, u32[]{:S(2)}) %collective-permute-start.1) | collective-permute-done | bytes 131104 | tf_op jit(solution)/shard_map/ppermute | solution.py:319
  14.4 0.9 collective-permute-start.3
  15.3 7.9 %attend_first.1 = (f32[2,2048,128]{2,1,0:T(8,128)}, f32[2,2048,256]{2,1,0:T(8,128)}) custom-call(s32[66]{0:T(128)} %pad_add_fusion.table.refs_0_, bf16[256,2048]{1,0:T(8,128)(2,1)} %q_ref.3, bf16[4,2,128,128]{3,2,1,0:T(8,128)(2,1)} %copy-done.6, bf16[4,2,128,128]{3,2,1,0:T(8,128)(2,1)} %copy-done.5), custom_call_target="tpu_custom_call" | custom-call | flops 4294967296 | bytes 8388608 | tf_op jit(solution)/shard_map/attend_first/pallas_call | solution.py:336
  23.2 0.1 pad_maximum_fusion.3
  23.3 0.1 pad_maximum_fusion.2
  23.4 1.3 %collective-permute-start.5 = (bf16[8,2,128,128]{3,2,1,0:T(8,128)(2,1)S(1)}, bf16[8,2,128,128]{3,2,1,0:T(8,128)(2,1)S(1)}, u32[]{:S(2)}, u32[]{:S(2)}) collective-permute-start(bf16[8,2,128,128]{3,2,1,0:T(8,128)(2,1)S(1)} %pad_maximum_fusion.2), channel_id=1, source_target_pairs={{0,32},{1,5},{4,36},{5,1},{8,40},{9,13},{12,44},{13,9},{32,0},{33,... | collective-permute-start | bytes 1572872 | tf_op jit(solution)/shard_map/ppermute | solution.py:319
  24.7 1.8 %collective-permute-start.6 = (bf16[8,2,128,128]{3,2,1,0:T(8,128)(2,1)S(1)}, bf16[8,2,128,128]{3,2,1,0:T(8,128)(2,1)S(1)}, u32[]{:S(2)}, u32[]{:S(2)}) collective-permute-start(bf16[8,2,128,128]{3,2,1,0:T(8,128)(2,1)S(1)} %pad_maximum_fusion.3), channel_id=1, source_target_pairs={{0,96},{1,13},{4,100},{5,9},{8,104},{9,5},{12,108},{13,1},{32,64},... | collective-permute-start | bytes 1572872 | tf_op jit(solution)/shard_map/ppermute | solution.py:319
  26.5 9.6 %attend_second.1.refs_3_ = f32[2,2048,256]{2,1,0:T(8,128)} custom-call(s32[66]{0:T(128)} %pad_add_fusion.table.refs_0_, bf16[256,2048]{1,0:T(8,128)(2,1)} %q_ref.3, f32[2,2048,128]{2,1,0:T(8,128)} %get-tuple-element.14.refs_2_.top_in, f32[2,2048,256]{2,1,0:T(8,128)} %get-tuple-element.18.refs_3_, bf16[4,2,128,128]{3,2,1,0:T(8,128)(2,1)} %copy-done.8, ...), custom_call_target="tpu_custom_call" | custom-call | flops 4294967296 | bytes 8388608 | tf_op jit(solution)/shard_map/attend_second/pallas_call | solution.py:300
  36.1 0.1 pad_maximum_fusion.sa
  36.3 0.1 pad_maximum_fusion.1.sb
  36.4 0.9 %collective-permute-start.7 = (bf16[16,2,128,128]{3,2,1,0:T(8,128)(2,1)S(1)}, bf16[16,2,128,128]{3,2,1,0:T(8,128)(2,1)S(1)}, u32[]{:S(2)}, u32[]{:S(2)}) collective-permute-start(bf16[16,2,128,128]{3,2,1,0:T(8,128)(2,1)S(1)} %pad_maximum_fusion.sa), channel_id=1, source_target_pairs={{0,96},{1,13},{4,100},{5,9},{8,104},{9,5},{12,108},{13,1},{32,64},... | collective-permute-start | bytes 3145736 | tf_op jit(solution)/shard_map/ppermute | solution.py:319
  37.3 14.2 %attend_third.1.refs_3_ = f32[2,2048,256]{2,1,0:T(8,128)} custom-call(s32[66]{0:T(128)} %pad_add_fusion.table.refs_0_, bf16[256,2048]{1,0:T(8,128)(2,1)} %q_ref.3, f32[2,2048,128]{2,1,0:T(8,128)} %get-tuple-element.14.refs_2_.top_in, f32[2,2048,256]{2,1,0:T(8,128)} %attend_second.1.refs_3_, bf16[8,2,128,128]{3,2,1,0:T(8,128)(2,1)} %copy-done.3, ...), custom_call_target="tpu_custom_call" | custom-call | flops 8589934592 | bytes 8388608 | tf_op jit(solution)/shard_map/attend_third/pallas_call | solution.py:300
  51.5 0.1 collective-permute-done.7.refs_4_.ra
  51.6 1.0 %copy-done.2 = bf16[16,2,128,128]{3,2,1,0:T(8,128)(2,1)} copy-done((bf16[16,2,128,128]{3,2,1,0:T(8,128)(2,1)}, bf16[16,2,128,128]{3,2,1,0:T(8,128)(2,1)S(1)}, u32[]{:S(2)}) %copy-start.2) | copy-done | bytes 1048600
  52.6 2.2 %pick_pages.1.mine = bf16[2,2,128,128]{3,2,1,0:T(8,128)(2,1)} custom-call(s32[66]{0:T(128)} %pad_add_fusion.table.refs_0_, bf16[16,2,128,128]{3,2,1,0:T(8,128)(2,1)} %copy-done, bf16[16,2,128,128]{3,2,1,0:T(8,128)(2,1)} %copy-done.2, bf16[16,2,128,128]{3,2,1,0:T(8,128)(2,1)} %copy-done.1, bf16[16,2,128,128]{3,2,1,0:T(8,128)(2,1)} %collective-permute-done.8.rb.b_ref), custom_call_target="tpu_custom_call" | custom-call | tf_op jit(solution)/shard_map/pick_pages/pallas_call | solution.py:354
  54.8 7.5 %collective-permute-start.11 = (bf16[2,2,128,128]{3,2,1,0:T(8,128)(2,1)}, bf16[2,2,128,128]{3,2,1,0:T(8,128)(2,1)S(1)}, u32[]{:S(2)}, u32[]{:S(2)}) collective-permute-start(bf16[2,2,128,128]{3,2,1,0:T(8,128)(2,1)} %pick_pages.1.mine), channel_id=1, source_target_pairs={{0,3},{1,2},{2,1},{3,0},{4,7},{5,6},{6,5},{7,4},{8,11},{9,10},{10,... | collective-permute-start | bytes 393224 | tf_op jit(solution)/shard_map/ppermute | solution.py:363
  62.3 0.5 collective-permute-start.9
  62.8 14.2 %attend_fourth.1.acc_in = f32[2,2048,256]{2,1,0:T(8,128)} custom-call(s32[66]{0:T(128)} %pad_add_fusion.table.refs_0_, bf16[256,2048]{1,0:T(8,128)(2,1)} %q_ref.3, f32[2,2048,128]{2,1,0:T(8,128)} %get-tuple-element.14.refs_2_.top_in, f32[2,2048,256]{2,1,0:T(8,128)} %attend_third.1.refs_3_, bf16[16,2,128,128]{3,2,1,0:T(8,128)(2,1)} %copy-done.2), custom_call_target="tpu_custom_call" | custom-call | flops 8589934592 | bytes 8388608 | tf_op jit(solution)/shard_map/attend_fourth/pallas_call | solution.py:300
  77.0 0.6 copy-done.9
  77.6 0.1 copy-done.10
  77.6 0.7 copy-done.11
  78.3 14.3 %attend_last.1 = (bf16[256,2048]{1,0:T(8,128)(2,1)}, bf16[2,4,2,128,128]{4,3,2,1,0:T(8,128)(2,1)}, f32[2,2,4]{2,1,0:T(2,128)}) custom-call(s32[66]{0:T(128)} %pad_add_fusion.table.refs_0_, bf16[256,2048]{1,0:T(8,128)(2,1)} %q_ref.3, f32[2,2048,128]{2,1,0:T(8,128)} %get-tuple-element.14.refs_2_.top_in, f32[2,2048,256]{2,1,0:T(8,128)} %attend_fourth.1.acc_in, ...), custom_call_target="tpu_custom_call" | custom-call | flops 8589934592 | bytes 8388608 | tf_op jit(solution)/shard_map/attend_last/pallas_call | solution.py:366
  (35 shorter events, 0.2 us)
Async XLA Ops:
  1.5 5.7 %collective-permute-start = (bf16[2,1,2,128,128]{4,3,2,1,0:T(8,128)(2,1)S(1)}, bf16[2,1,2,128,128]{4,3,2,1,0:T(8,128)(2,1)S(1)}, u32[]{:S(2)}, u32[]{:S(2)}) collective-permute-start(bf16[2,1,2,128,128]{4,3,2,1,0:T(8,128)(2,1)S(1)} %maximum_bitcast_fusion), channel_id=1, source_target_pairs={{0,16},{16,0},{1,17},{17,1},{2,18},{18,2},{3,19},{19,3},{4,20},{20... | collective-permute-start | bytes 393224 | tf_op jit(solution)/shard_map/ppermute | solution.py:324
  7.3 5.1 %collective-permute-start.2 = (bf16[2,2,128,128]{3,2,1,0:T(8,128)(2,1)S(1)}, bf16[2,2,128,128]{3,2,1,0:T(8,128)(2,1)S(1)}, u32[]{:S(2)}, u32[]{:S(2)}) collective-permute-start(bf16[2,2,128,128]{3,2,1,0:T(8,128)(2,1)S(1)} %get-tuple-element.27), channel_id=1, source_target_pairs={{0,12},{1,97},{4,8},{5,101},{8,4},{9,105},{12,0},{13,109},{32,44},... | collective-permute-start | bytes 393224 | tf_op jit(solution)/shard_map/ppermute | solution.py:319
  10.2 4.2 %collective-permute-start.1 = (bf16[2,2,128,128]{3,2,1,0:T(8,128)(2,1)S(1)}, bf16[2,2,128,128]{3,2,1,0:T(8,128)(2,1)S(1)}, u32[]{:S(2)}, u32[]{:S(2)}) collective-permute-start(bf16[2,2,128,128]{3,2,1,0:T(8,128)(2,1)S(1)} %get-tuple-element.28), channel_id=1, source_target_pairs={{0,4},{1,33},{4,0},{5,37},{8,12},{9,41},{12,8},{13,45},{32,36},{33... | collective-permute-start | bytes 393224 | tf_op jit(solution)/shard_map/ppermute | solution.py:319
  12.4 2.9 %copy-start.5 = (bf16[4,2,128,128]{3,2,1,0:T(8,128)(2,1)}, bf16[4,2,128,128]{3,2,1,0:T(8,128)(2,1)S(1)}, u32[]{:S(2)}) copy-start(bf16[4,2,128,128]{3,2,1,0:T(8,128)(2,1)S(1)} %pad_maximum_fusion.5.b_ref) | copy-start | bytes 786436
  12.4 10.8 %collective-permute-start.4 = (bf16[4,2,128,128]{3,2,1,0:T(8,128)(2,1)S(1)}, bf16[4,2,128,128]{3,2,1,0:T(8,128)(2,1)S(1)}, u32[]{:S(2)}, u32[]{:S(2)}) collective-permute-start(bf16[4,2,128,128]{3,2,1,0:T(8,128)(2,1)S(1)} %pad_maximum_fusion.5.b_ref), channel_id=1, source_target_pairs={{0,4},{1,33},{4,0},{5,37},{8,12},{9,41},{12,8},{13,45},{32,36},{33... | collective-permute-start | bytes 786440 | tf_op jit(solution)/shard_map/ppermute | solution.py:319
  14.4 0.9 copy-start.6
  14.4 8.9 %collective-permute-start.3 = (bf16[4,2,128,128]{3,2,1,0:T(8,128)(2,1)S(1)}, bf16[4,2,128,128]{3,2,1,0:T(8,128)(2,1)S(1)}, u32[]{:S(2)}, u32[]{:S(2)}) collective-permute-start(bf16[4,2,128,128]{3,2,1,0:T(8,128)(2,1)S(1)} %pad_maximum_fusion.4.a_ref), channel_id=1, source_target_pairs={{0,12},{1,97},{4,8},{5,101},{8,4},{9,105},{12,0},{13,109},{32,44},... | collective-permute-start | bytes 786440 | tf_op jit(solution)/shard_map/ppermute | solution.py:319
  23.2 3.3 %copy-start.7 = (bf16[4,2,128,128]{3,2,1,0:T(8,128)(2,1)}, bf16[4,2,128,128]{3,2,1,0:T(8,128)(2,1)S(1)}, u32[]{:S(2)}) copy-start(bf16[4,2,128,128]{3,2,1,0:T(8,128)(2,1)S(1)} %collective-permute-done.4.refs_5_) | copy-start | bytes 786436
  23.3 3.2 %copy-start.8 = (bf16[4,2,128,128]{3,2,1,0:T(8,128)(2,1)}, bf16[4,2,128,128]{3,2,1,0:T(8,128)(2,1)S(1)}, u32[]{:S(2)}) copy-start(bf16[4,2,128,128]{3,2,1,0:T(8,128)(2,1)S(1)} %collective-permute-done.3.refs_4_) | copy-start | bytes 786436
  23.4 12.7 %collective-permute-start.5 = (bf16[8,2,128,128]{3,2,1,0:T(8,128)(2,1)S(1)}, bf16[8,2,128,128]{3,2,1,0:T(8,128)(2,1)S(1)}, u32[]{:S(2)}, u32[]{:S(2)}) collective-permute-start(bf16[8,2,128,128]{3,2,1,0:T(8,128)(2,1)S(1)} %pad_maximum_fusion.2), channel_id=1, source_target_pairs={{0,32},{1,5},{4,36},{5,1},{8,40},{9,13},{12,44},{13,9},{32,0},{33,... | collective-permute-start | bytes 1572872 | tf_op jit(solution)/shard_map/ppermute | solution.py:319
  24.7 11.5 %collective-permute-start.6 = (bf16[8,2,128,128]{3,2,1,0:T(8,128)(2,1)S(1)}, bf16[8,2,128,128]{3,2,1,0:T(8,128)(2,1)S(1)}, u32[]{:S(2)}, u32[]{:S(2)}) collective-permute-start(bf16[8,2,128,128]{3,2,1,0:T(8,128)(2,1)S(1)} %pad_maximum_fusion.3), channel_id=1, source_target_pairs={{0,96},{1,13},{4,100},{5,9},{8,104},{9,5},{12,108},{13,1},{32,64},... | collective-permute-start | bytes 1572872 | tf_op jit(solution)/shard_map/ppermute | solution.py:319
  36.1 1.2 %copy-start.3 = (bf16[8,2,128,128]{3,2,1,0:T(8,128)(2,1)}, bf16[8,2,128,128]{3,2,1,0:T(8,128)(2,1)S(1)}, u32[]{:S(2)}) copy-start(bf16[8,2,128,128]{3,2,1,0:T(8,128)(2,1)S(1)} %collective-permute-done.5.refs_4_) | copy-start | bytes 1572868
  36.2 15.3 %copy-start = (bf16[16,2,128,128]{3,2,1,0:T(8,128)(2,1)}, bf16[16,2,128,128]{3,2,1,0:T(8,128)(2,1)S(1)}, u32[]{:S(2)}) copy-start(bf16[16,2,128,128]{3,2,1,0:T(8,128)(2,1)S(1)} %pad_maximum_fusion.sa) | copy-start | bytes 3145732
  36.2 1.1 %copy-start.4 = (bf16[8,2,128,128]{3,2,1,0:T(8,128)(2,1)}, bf16[8,2,128,128]{3,2,1,0:T(8,128)(2,1)S(1)}, u32[]{:S(2)}) copy-start(bf16[8,2,128,128]{3,2,1,0:T(8,128)(2,1)S(1)} %collective-permute-done.6.refs_5_) | copy-start | bytes 1572868
  36.4 15.2 %copy-start.1 = (bf16[16,2,128,128]{3,2,1,0:T(8,128)(2,1)}, bf16[16,2,128,128]{3,2,1,0:T(8,128)(2,1)S(1)}, u32[]{:S(2)}) copy-start(bf16[16,2,128,128]{3,2,1,0:T(8,128)(2,1)S(1)} %pad_maximum_fusion.1.sb) | copy-start | bytes 3145732
  36.4 15.2 %collective-permute-start.7 = (bf16[16,2,128,128]{3,2,1,0:T(8,128)(2,1)S(1)}, bf16[16,2,128,128]{3,2,1,0:T(8,128)(2,1)S(1)}, u32[]{:S(2)}, u32[]{:S(2)}) collective-permute-start(bf16[16,2,128,128]{3,2,1,0:T(8,128)(2,1)S(1)} %pad_maximum_fusion.sa), channel_id=1, source_target_pairs={{0,96},{1,13},{4,100},{5,9},{8,104},{9,5},{12,108},{13,1},{32,64},... | collective-permute-start | bytes 3145736 | tf_op jit(solution)/shard_map/ppermute | solution.py:319
  37.3 14.3 %collective-permute-start.8 = (bf16[16,2,128,128]{3,2,1,0:T(8,128)(2,1)S(1)}, bf16[16,2,128,128]{3,2,1,0:T(8,128)(2,1)}, u32[]{:S(2)}, u32[]{:S(2)}) collective-permute-start(bf16[16,2,128,128]{3,2,1,0:T(8,128)(2,1)S(1)} %pad_maximum_fusion.1.sb), channel_id=1, source_target_pairs={{0,32},{1,5},{4,36},{5,1},{8,40},{9,13},{12,44},{13,9},{32,0},{33,... | collective-permute-start | bytes 3145736 | tf_op jit(solution)/shard_map/ppermute | solution.py:319
  51.6 1.0 %copy-start.2 = (bf16[16,2,128,128]{3,2,1,0:T(8,128)(2,1)}, bf16[16,2,128,128]{3,2,1,0:T(8,128)(2,1)S(1)}, u32[]{:S(2)}) copy-start(bf16[16,2,128,128]{3,2,1,0:T(8,128)(2,1)S(1)} %collective-permute-done.7.refs_4_.ra) | copy-start | bytes 3145732
  54.8 22.1 %collective-permute-start.11 = (bf16[2,2,128,128]{3,2,1,0:T(8,128)(2,1)}, bf16[2,2,128,128]{3,2,1,0:T(8,128)(2,1)S(1)}, u32[]{:S(2)}, u32[]{:S(2)}) collective-permute-start(bf16[2,2,128,128]{3,2,1,0:T(8,128)(2,1)} %pick_pages.1.mine), channel_id=1, source_target_pairs={{0,3},{1,2},{2,1},{3,0},{4,7},{5,6},{6,5},{7,4},{8,11},{9,10},{10,... | collective-permute-start | bytes 393224 | tf_op jit(solution)/shard_map/ppermute | solution.py:363
  62.3 14.7 %collective-permute-start.10 = (bf16[2,2,128,128]{3,2,1,0:T(8,128)(2,1)}, bf16[2,2,128,128]{3,2,1,0:T(8,128)(2,1)S(1)}, u32[]{:S(2)}, u32[]{:S(2)}) collective-permute-start(bf16[2,2,128,128]{3,2,1,0:T(8,128)(2,1)} %pick_pages.1.mine), channel_id=1, source_target_pairs={{0,2},{1,3},{2,0},{3,1},{4,6},{5,7},{6,4},{7,5},{8,10},{9,11},{10,... | collective-permute-start | bytes 393224 | tf_op jit(solution)/shard_map/ppermute | solution.py:363
  62.3 14.7 %collective-permute-start.9 = (bf16[2,2,128,128]{3,2,1,0:T(8,128)(2,1)}, bf16[2,2,128,128]{3,2,1,0:T(8,128)(2,1)S(1)}, u32[]{:S(2)}, u32[]{:S(2)}) collective-permute-start(bf16[2,2,128,128]{3,2,1,0:T(8,128)(2,1)} %pick_pages.1.mine), channel_id=1, source_target_pairs={{0,1},{1,0},{2,3},{3,2},{4,5},{5,4},{6,7},{7,6},{8,9},{9,8},{10,11... | collective-permute-start | bytes 393224 | tf_op jit(solution)/shard_map/ppermute | solution.py:363
  76.9 0.6 copy-start.9
  77.0 0.7 copy-start.10
  77.6 0.7 copy-start.11

commit v2 on v1

--- a/solution.py
+++ b/solution.py
@@ -12,6 +12,8 @@
 SCALE2 = DH ** (-0.5) * 1.4426950408889634
 TILE = 4
 LIMIT = 2.0**100
+FRONT = pl.ds(0, ROWS - TILE * SP)
+BACK = pl.ds(ROWS - TILE * SP, TILE * SP)
 NT = (((1,), (1,)), ((), ()))
 MASKS = ((1, 3), (3, 1))
 PIECES = 32
@@ -72,6 +74,14 @@
 
 def tile_rows(tile):
     return slice(tile * TILE * SP, (tile + 1) * TILE * SP)
+
+
+def leaving(sems, s, piece, *pairs):
+    rows = (FRONT, BACK)[piece]
+    return [
+        pltpu.make_async_copy(ref.at[s, rows], out.at[s, rows], sems.at[2 * piece + k, s])
+        for k, (ref, out) in enumerate(pairs)
+    ]
 
 
 def first_kernel(table, q_ref, a_ref, b_ref, top_out, acc_out, top_ref, acc, sems):
@@ -98,14 +108,18 @@
             near = jnp.where(keep, jnp.exp2(diagonal - top), 0.0).astype(jnp.bfloat16)
             weight = jnp.concatenate([near, weigh(score[:, SP:], top, len(ks) + 1)], axis=1)
             acc[s, at, :] = jnp.dot(weight, vg, preferred_element_type=jnp.float32)
-        for k, (ref, out) in enumerate(((top_ref, top_out), (acc, acc_out))):
-            pltpu.make_async_copy(ref.at[s], out.at[s], sems.at[k, s]).start()
+            if tile == HEADS // TILE - 2:
+                for copy in leaving(sems, s, 0, (top_ref, top_out), (acc, acc_out)):
+                    copy.start()
+        for copy in leaving(sems, s, 1, (top_ref, top_out), (acc, acc_out)):
+            copy.start()
         return carry
 
     lax.fori_loop(0, 2, span, 0)
     for s in range(2):
-        for k, (ref, out) in enumerate(((top_ref, top_out), (acc, acc_out))):
-            pltpu.make_async_copy(ref.at[s], out.at[s], sems.at[k, s]).wait()
+        for piece in range(2):
+            for copy in leaving(sems, s, piece, (top_ref, top_out), (acc, acc_out)):
+                copy.wait()
 
 
 def span_sums(s, table, q_ref, parts, top_ref, store):
@@ -123,25 +137,32 @@
     *pieces, acc_out, top_ref, acc, sems = refs
     parts = tuple(zip(pieces, firsts))
     ins = ((top_in, top_ref), (acc_in, acc))
-    for s in range(2):
-        for k, (i, o) in enumerate(ins):
-            pltpu.make_async_copy(i.at[s], o.at[s], sems.at[k, s]).start()
+    for k, (i, o) in enumerate(ins):
+        pltpu.make_async_copy(i.at[0], o.at[0], sems.at[k, 0]).start()
 
     def span(s, carry):
         for k, (i, o) in enumerate(ins):
             pltpu.make_async_copy(i.at[s], o.at[s], sems.at[k, s]).wait()
 
+        @pl.when(s == 0)
+        def _():
+            for k, (i, o) in enumerate(ins):
+                pltpu.make_async_copy(i.at[1], o.at[1], sems.at[k, 1]).start()
+
         def store(tile, sums):
             at = tile_rows(tile)
             acc[s, at, :] = acc[s, at, :] + sums
+            if tile == HEADS // TILE - 2:
+                pltpu.make_async_copy(acc.at[s, FRONT], acc_out.at[s, FRONT], sems.at[2, s]).start()
 
         span_sums(s, table, q_ref, parts, top_ref, store)
-        pltpu.make_async_copy(acc.at[s], acc_out.at[s], sems.at[2, s]).start()
+        pltpu.make_async_copy(acc.at[s, BACK], acc_out.at[s, BACK], sems.at[3, s]).start()
         return carry
 
     lax.fori_loop(0, 2, span, 0)
     for s in range(2):
-        pltpu.make_async_copy(acc.at[s], acc_out.at[s], sems.at[2, s]).wait()
+        pltpu.make_async_copy(acc.at[s, FRONT], acc_out.at[s, FRONT], sems.at[2, s]).wait()
+        pltpu.make_async_copy(acc.at[s, BACK], acc_out.at[s, BACK], sems.at[3, s]).wait()
 
 
 def last_kernel(
@@ -292,7 +313,7 @@
     return [
         pltpu.VMEM(TOPS, jnp.float32),
         pltpu.VMEM(SUMS, jnp.float32),
-        pltpu.SemaphoreType.DMA((3, 2)),
+        pltpu.SemaphoreType.DMA((4, 2)),
     ]
 
 

time: 93.1 us -> 91.7 us (0.985)
  Pallas kernels: 62.3 us -> 60.3 us
    pallas_call x3, Pallas kernels: 37.9 us -> 36.4 us  [sums_of(): pl.pallas_call(lambda *refs: next_kernel(firsts, *refs), out_shape=f32(*S...]
  transfers between devices with their start and end apart: 12 -> 12, of which waited for: 4 -> 4; matrix products, arithmetic and copies ran while one was open for 2% -> 2% of each run, Pallas kernels for 49% -> 48%
where the time goes in v2:
time: 91.7 us; the launch traced here: 91.3 us
  Pallas kernels  60.3 us (66%)
  starting transfers between devices  18.3 us (20%)
  waiting for transfers between devices  6.23 us (7%)
  other arithmetic  2.97 us (3%)
  local copies, waits for them, and re-layouts  2.33 us (3%)
  between operations  1.09 us (1%)
    pallas_call x3, Pallas kernels, sums_of(): pl.pallas_call(lambda *refs: next_kernel(firsts, *refs), out_shape=f32(*S...  36.4 us
    pallas_call x1, Pallas kernels, on_device(): pl.pallas_call(last_kernel, out_shape=(bf16(2 * SP, HEADS * DH), bf16(2,...  14.3 us
    ppermute x3, starting transfers between devices, on_device(): lax.ppermute(mine, ('zh', 'core'), [(i, i ^ away) for i in range(4)])  7.98 us
    ppermute x8, starting transfers between devices, swap(): return lax.ppermute(x, ('y', 'x', 'core'), pairs)  7.82 us
    pallas_call x1, Pallas kernels, on_device(): pl.pallas_call(first_kernel, out_shape=(f32(*TOPS), f32(*SUMS)), in_specs...  7.46 us
    ppermute x8, waiting for transfers between devices, swap(): return lax.ppermute(x, ('y', 'x', 'core'), pairs)  3.9 us
    ppermute x1, starting transfers between devices, on_device(): lax.ppermute(own, 'zl', [(0, 1), (1, 0)])  2.55 us
    unnamed x24, local copies, waits for them, and re-layouts  2.33 us
  transfers between devices with their start and end apart: 12, of which 4 were waited for; matrix products, arithmetic and copies ran while one was open for 2% of the time, Pallas kernels for 48%

profile of v2, /device:TPU:1, one launch (start us, length us, event | category | flops | bytes accessed | tf_op | source)
XLA Modules:
  0.0 91.3 jit_solution(16441098185441672214)
XLA Ops:
  0.6 0.9 maximum_bitcast_fusion
  1.5 2.5 %collective-permute-start = (bf16[2,1,2,128,128]{4,3,2,1,0:T(8,128)(2,1)S(1)}, bf16[2,1,2,128,128]{4,3,2,1,0:T(8,128)(2,1)S(1)}, u32[]{:S(2)}, u32[]{:S(2)}) collective-permute-start(bf16[2,1,2,128,128]{4,3,2,1,0:T(8,128)(2,1)S(1)} %maximum_bitcast_fusion), channel_id=1, source_target_pairs={{0,16},{16,0},{1,17},{17,1},{2,18},{18,2},{3,19},{19,3},{4,20},{20... | collective-permute-start | bytes 393224 | tf_op jit(solution)/shard_map/ppermute | solution.py:345
  4.1 0.8 select_reduce_fusion.1
  5.0 2.3 %collective-permute-done = bf16[2,1,2,128,128]{4,3,2,1,0:T(8,128)(2,1)S(1)} collective-permute-done((bf16[2,1,2,128,128]{4,3,2,1,0:T(8,128)(2,1)S(1)}, bf16[2,1,2,128,128]{4,3,2,1,0:T(8,128)(2,1)S(1)}, u32[]{:S(2)}, u32[]{:S(2)}) %collective-permute-start) | collective-permute-done | bytes 131104 | tf_op jit(solution)/shard_map/ppermute | solution.py:345
  7.3 2.7 %collective-permute-start.2 = (bf16[2,2,128,128]{3,2,1,0:T(8,128)(2,1)S(1)}, bf16[2,2,128,128]{3,2,1,0:T(8,128)(2,1)S(1)}, u32[]{:S(2)}, u32[]{:S(2)}) collective-permute-start(bf16[2,2,128,128]{3,2,1,0:T(8,128)(2,1)S(1)} %get-tuple-element.27), channel_id=1, source_target_pairs={{0,12},{1,97},{4,8},{5,101},{8,4},{9,105},{12,0},{13,109},{32,44},... | collective-permute-start | bytes 393224 | tf_op jit(solution)/shard_map/ppermute | solution.py:340
  10.0 0.2 fusion.3
  10.2 0.1 collective-permute-start.1
  10.3 0.7 pad_add_fusion.table.refs_0_
  10.9 1.5 %collective-permute-done.2 = bf16[2,2,128,128]{3,2,1,0:T(8,128)(2,1)S(1)} collective-permute-done((bf16[2,2,128,128]{3,2,1,0:T(8,128)(2,1)S(1)}, bf16[2,2,128,128]{3,2,1,0:T(8,128)(2,1)S(1)}, u32[]{:S(2)}, u32[]{:S(2)}) %collective-permute-start.2) | collective-permute-done | bytes 131104 | tf_op jit(solution)/shard_map/ppermute | solution.py:340
  12.4 0.1 collective-permute-start.4
  12.5 1.8 %collective-permute-done.1 = bf16[2,2,128,128]{3,2,1,0:T(8,128)(2,1)S(1)} collective-permute-done((bf16[2,2,128,128]{3,2,1,0:T(8,128)(2,1)S(1)}, bf16[2,2,128,128]{3,2,1,0:T(8,128)(2,1)S(1)}, u32[]{:S(2)}, u32[]{:S(2)}) %collective-permute-start.1) | collective-permute-done | bytes 131104 | tf_op jit(solution)/shard_map/ppermute | solution.py:340
  14.4 0.9 collective-permute-start.3
  15.3 7.5 %attend_first.1 = (f32[2,2048,128]{2,1,0:T(8,128)}, f32[2,2048,256]{2,1,0:T(8,128)}) custom-call(s32[66]{0:T(128)} %pad_add_fusion.table.refs_0_, bf16[256,2048]{1,0:T(8,128)(2,1)} %q_ref.3, bf16[4,2,128,128]{3,2,1,0:T(8,128)(2,1)} %copy-done.6, bf16[4,2,128,128]{3,2,1,0:T(8,128)(2,1)} %copy-done.5), custom_call_target="tpu_custom_call" | custom-call | flops 4294967296 | bytes 8388608 | tf_op jit(solution)/shard_map/attend_first/pallas_call | solution.py:357
  22.8 0.1 pad_maximum_fusion.3
  22.9 0.1 pad_maximum_fusion.2
  23.0 1.3 %collective-permute-start.5 = (bf16[8,2,128,128]{3,2,1,0:T(8,128)(2,1)S(1)}, bf16[8,2,128,128]{3,2,1,0:T(8,128)(2,1)S(1)}, u32[]{:S(2)}, u32[]{:S(2)}) collective-permute-start(bf16[8,2,128,128]{3,2,1,0:T(8,128)(2,1)S(1)} %pad_maximum_fusion.2), channel_id=1, source_target_pairs={{0,32},{1,5},{4,36},{5,1},{8,40},{9,13},{12,44},{13,9},{32,0},{33,... | collective-permute-start | bytes 1572872 | tf_op jit(solution)/shard_map/ppermute | solution.py:340
  24.3 1.8 %collective-permute-start.6 = (bf16[8,2,128,128]{3,2,1,0:T(8,128)(2,1)S(1)}, bf16[8,2,128,128]{3,2,1,0:T(8,128)(2,1)S(1)}, u32[]{:S(2)}, u32[]{:S(2)}) collective-permute-start(bf16[8,2,128,128]{3,2,1,0:T(8,128)(2,1)S(1)} %pad_maximum_fusion.3), channel_id=1, source_target_pairs={{0,96},{1,13},{4,100},{5,9},{8,104},{9,5},{12,108},{13,1},{32,64},... | collective-permute-start | bytes 1572872 | tf_op jit(solution)/shard_map/ppermute | solution.py:340
  26.1 9.1 %attend_second.1.refs_3_ = f32[2,2048,256]{2,1,0:T(8,128)} custom-call(s32[66]{0:T(128)} %pad_add_fusion.table.refs_0_, bf16[256,2048]{1,0:T(8,128)(2,1)} %q_ref.3, f32[2,2048,128]{2,1,0:T(8,128)} %get-tuple-element.14.refs_2_.top_in, f32[2,2048,256]{2,1,0:T(8,128)} %get-tuple-element.18.refs_3_, bf16[4,2,128,128]{3,2,1,0:T(8,128)(2,1)} %copy-done.8, ...), custom_call_target="tpu_custom_call" | custom-call | flops 4294967296 | bytes 8388608 | tf_op jit(solution)/shard_map/attend_second/pallas_call | solution.py:321
  35.2 0.1 pad_maximum_fusion.sa
  35.3 0.1 pad_maximum_fusion.1.sb
  35.4 0.9 %collective-permute-start.7 = (bf16[16,2,128,128]{3,2,1,0:T(8,128)(2,1)S(1)}, bf16[16,2,128,128]{3,2,1,0:T(8,128)(2,1)S(1)}, u32[]{:S(2)}, u32[]{:S(2)}) collective-permute-start(bf16[16,2,128,128]{3,2,1,0:T(8,128)(2,1)S(1)} %pad_maximum_fusion.sa), channel_id=1, source_target_pairs={{0,96},{1,13},{4,100},{5,9},{8,104},{9,5},{12,108},{13,1},{32,64},... | collective-permute-start | bytes 3145736 | tf_op jit(solution)/shard_map/ppermute | solution.py:340
  36.4 13.7 %attend_third.1.refs_3_ = f32[2,2048,256]{2,1,0:T(8,128)} custom-call(s32[66]{0:T(128)} %pad_add_fusion.table.refs_0_, bf16[256,2048]{1,0:T(8,128)(2,1)} %q_ref.3, f32[2,2048,128]{2,1,0:T(8,128)} %get-tuple-element.14.refs_2_.top_in, f32[2,2048,256]{2,1,0:T(8,128)} %attend_second.1.refs_3_, bf16[8,2,128,128]{3,2,1,0:T(8,128)(2,1)} %copy-done.3, ...), custom_call_target="tpu_custom_call" | custom-call | flops 8589934592 | bytes 8388608 | tf_op jit(solution)/shard_map/attend_third/pallas_call | solution.py:321
  50.1 0.6 collective-permute-done.7.refs_4_.ra
  50.7 1.0 %copy-done.2 = bf16[16,2,128,128]{3,2,1,0:T(8,128)(2,1)} copy-done((bf16[16,2,128,128]{3,2,1,0:T(8,128)(2,1)}, bf16[16,2,128,128]{3,2,1,0:T(8,128)(2,1)S(1)}, u32[]{:S(2)}) %copy-start.2) | copy-done | bytes 1048600
  51.6 2.2 %pick_pages.1.mine = bf16[2,2,128,128]{3,2,1,0:T(8,128)(2,1)} custom-call(s32[66]{0:T(128)} %pad_add_fusion.table.refs_0_, bf16[16,2,128,128]{3,2,1,0:T(8,128)(2,1)} %copy-done, bf16[16,2,128,128]{3,2,1,0:T(8,128)(2,1)} %copy-done.2, bf16[16,2,128,128]{3,2,1,0:T(8,128)(2,1)} %copy-done.1, bf16[16,2,128,128]{3,2,1,0:T(8,128)(2,1)} %collective-permute-done.8.rb.b_ref), custom_call_target="tpu_custom_call" | custom-call | tf_op jit(solution)/shard_map/pick_pages/pallas_call | solution.py:375
  53.9 7.5 %collective-permute-start.11 = (bf16[2,2,128,128]{3,2,1,0:T(8,128)(2,1)}, bf16[2,2,128,128]{3,2,1,0:T(8,128)(2,1)S(1)}, u32[]{:S(2)}, u32[]{:S(2)}) collective-permute-start(bf16[2,2,128,128]{3,2,1,0:T(8,128)(2,1)} %pick_pages.1.mine), channel_id=1, source_target_pairs={{0,3},{1,2},{2,1},{3,0},{4,7},{5,6},{6,5},{7,4},{8,11},{9,10},{10,... | collective-permute-start | bytes 393224 | tf_op jit(solution)/shard_map/ppermute | solution.py:384
  61.4 0.5 collective-permute-start.9
  61.8 13.7 %attend_fourth.1.acc_in = f32[2,2048,256]{2,1,0:T(8,128)} custom-call(s32[66]{0:T(128)} %pad_add_fusion.table.refs_0_, bf16[256,2048]{1,0:T(8,128)(2,1)} %q_ref.3, f32[2,2048,128]{2,1,0:T(8,128)} %get-tuple-element.14.refs_2_.top_in, f32[2,2048,256]{2,1,0:T(8,128)} %attend_third.1.refs_3_, bf16[16,2,128,128]{3,2,1,0:T(8,128)(2,1)} %copy-done.2), custom_call_target="tpu_custom_call" | custom-call | flops 8589934592 | bytes 8388608 | tf_op jit(solution)/shard_map/attend_fourth/pallas_call | solution.py:321
  75.5 0.6 copy-done.9
  76.1 0.1 copy-done.10
  76.2 0.7 copy-done.11
  76.9 14.3 %attend_last.1 = (bf16[256,2048]{1,0:T(8,128)(2,1)}, bf16[2,4,2,128,128]{4,3,2,1,0:T(8,128)(2,1)}, f32[2,2,4]{2,1,0:T(2,128)}) custom-call(s32[66]{0:T(128)} %pad_add_fusion.table.refs_0_, bf16[256,2048]{1,0:T(8,128)(2,1)} %q_ref.3, f32[2,2048,128]{2,1,0:T(8,128)} %get-tuple-element.14.refs_2_.top_in, f32[2,2048,256]{2,1,0:T(8,128)} %attend_fourth.1.acc_in, ...), custom_call_target="tpu_custom_call" | custom-call | flops 8589934592 | bytes 8388608 | tf_op jit(solution)/shard_map/attend_last/pallas_call | solution.py:387
  (35 shorter events, 0.2 us)
Async XLA Ops:
  1.5 5.7 %collective-permute-start = (bf16[2,1,2,128,128]{4,3,2,1,0:T(8,128)(2,1)S(1)}, bf16[2,1,2,128,128]{4,3,2,1,0:T(8,128)(2,1)S(1)}, u32[]{:S(2)}, u32[]{:S(2)}) collective-permute-start(bf16[2,1,2,128,128]{4,3,2,1,0:T(8,128)(2,1)S(1)} %maximum_bitcast_fusion), channel_id=1, source_target_pairs={{0,16},{16,0},{1,17},{17,1},{2,18},{18,2},{3,19},{19,3},{4,20},{20... | collective-permute-start | bytes 393224 | tf_op jit(solution)/shard_map/ppermute | solution.py:345
  7.3 5.1 %collective-permute-start.2 = (bf16[2,2,128,128]{3,2,1,0:T(8,128)(2,1)S(1)}, bf16[2,2,128,128]{3,2,1,0:T(8,128)(2,1)S(1)}, u32[]{:S(2)}, u32[]{:S(2)}) collective-permute-start(bf16[2,2,128,128]{3,2,1,0:T(8,128)(2,1)S(1)} %get-tuple-element.27), channel_id=1, source_target_pairs={{0,12},{1,97},{4,8},{5,101},{8,4},{9,105},{12,0},{13,109},{32,44},... | collective-permute-start | bytes 393224 | tf_op jit(solution)/shard_map/ppermute | solution.py:340
  10.2 4.2 %collective-permute-start.1 = (bf16[2,2,128,128]{3,2,1,0:T(8,128)(2,1)S(1)}, bf16[2,2,128,128]{3,2,1,0:T(8,128)(2,1)S(1)}, u32[]{:S(2)}, u32[]{:S(2)}) collective-permute-start(bf16[2,2,128,128]{3,2,1,0:T(8,128)(2,1)S(1)} %get-tuple-element.28), channel_id=1, source_target_pairs={{0,4},{1,33},{4,0},{5,37},{8,12},{9,41},{12,8},{13,45},{32,36},{33... | collective-permute-start | bytes 393224 | tf_op jit(solution)/shard_map/ppermute | solution.py:340
  12.4 2.9 %copy-start.5 = (bf16[4,2,128,128]{3,2,1,0:T(8,128)(2,1)}, bf16[4,2,128,128]{3,2,1,0:T(8,128)(2,1)S(1)}, u32[]{:S(2)}) copy-start(bf16[4,2,128,128]{3,2,1,0:T(8,128)(2,1)S(1)} %pad_maximum_fusion.5.b_ref) | copy-start | bytes 786436
  12.4 10.3 %collective-permute-start.4 = (bf16[4,2,128,128]{3,2,1,0:T(8,128)(2,1)S(1)}, bf16[4,2,128,128]{3,2,1,0:T(8,128)(2,1)S(1)}, u32[]{:S(2)}, u32[]{:S(2)}) collective-permute-start(bf16[4,2,128,128]{3,2,1,0:T(8,128)(2,1)S(1)} %pad_maximum_fusion.5.b_ref), channel_id=1, source_target_pairs={{0,4},{1,33},{4,0},{5,37},{8,12},{9,41},{12,8},{13,45},{32,36},{33... | collective-permute-start | bytes 786440 | tf_op jit(solution)/shard_map/ppermute | solution.py:340
  14.4 0.9 copy-start.6
  14.4 8.5 %collective-permute-start.3 = (bf16[4,2,128,128]{3,2,1,0:T(8,128)(2,1)S(1)}, bf16[4,2,128,128]{3,2,1,0:T(8,128)(2,1)S(1)}, u32[]{:S(2)}, u32[]{:S(2)}) collective-permute-start(bf16[4,2,128,128]{3,2,1,0:T(8,128)(2,1)S(1)} %pad_maximum_fusion.4.a_ref), channel_id=1, source_target_pairs={{0,12},{1,97},{4,8},{5,101},{8,4},{9,105},{12,0},{13,109},{32,44},... | collective-permute-start | bytes 786440 | tf_op jit(solution)/shard_map/ppermute | solution.py:340
  22.8 3.3 %copy-start.7 = (bf16[4,2,128,128]{3,2,1,0:T(8,128)(2,1)}, bf16[4,2,128,128]{3,2,1,0:T(8,128)(2,1)S(1)}, u32[]{:S(2)}) copy-start(bf16[4,2,128,128]{3,2,1,0:T(8,128)(2,1)S(1)} %collective-permute-done.4.refs_5_) | copy-start | bytes 786436
  22.9 3.2 %copy-start.8 = (bf16[4,2,128,128]{3,2,1,0:T(8,128)(2,1)}, bf16[4,2,128,128]{3,2,1,0:T(8,128)(2,1)S(1)}, u32[]{:S(2)}) copy-start(bf16[4,2,128,128]{3,2,1,0:T(8,128)(2,1)S(1)} %collective-permute-done.3.refs_4_) | copy-start | bytes 786436
  23.0 12.2 %collective-permute-start.5 = (bf16[8,2,128,128]{3,2,1,0:T(8,128)(2,1)S(1)}, bf16[8,2,128,128]{3,2,1,0:T(8,128)(2,1)S(1)}, u32[]{:S(2)}, u32[]{:S(2)}) collective-permute-start(bf16[8,2,128,128]{3,2,1,0:T(8,128)(2,1)S(1)} %pad_maximum_fusion.2), channel_id=1, source_target_pairs={{0,32},{1,5},{4,36},{5,1},{8,40},{9,13},{12,44},{13,9},{32,0},{33,... | collective-permute-start | bytes 1572872 | tf_op jit(solution)/shard_map/ppermute | solution.py:340
  24.3 11.0 %collective-permute-start.6 = (bf16[8,2,128,128]{3,2,1,0:T(8,128)(2,1)S(1)}, bf16[8,2,128,128]{3,2,1,0:T(8,128)(2,1)S(1)}, u32[]{:S(2)}, u32[]{:S(2)}) collective-permute-start(bf16[8,2,128,128]{3,2,1,0:T(8,128)(2,1)S(1)} %pad_maximum_fusion.3), channel_id=1, source_target_pairs={{0,96},{1,13},{4,100},{5,9},{8,104},{9,5},{12,108},{13,1},{32,64},... | collective-permute-start | bytes 1572872 | tf_op jit(solution)/shard_map/ppermute | solution.py:340
  35.2 1.2 %copy-start.3 = (bf16[8,2,128,128]{3,2,1,0:T(8,128)(2,1)}, bf16[8,2,128,128]{3,2,1,0:T(8,128)(2,1)S(1)}, u32[]{:S(2)}) copy-start(bf16[8,2,128,128]{3,2,1,0:T(8,128)(2,1)S(1)} %collective-permute-done.5.refs_4_) | copy-start | bytes 1572868
  35.3 14.8 %copy-start = (bf16[16,2,128,128]{3,2,1,0:T(8,128)(2,1)}, bf16[16,2,128,128]{3,2,1,0:T(8,128)(2,1)S(1)}, u32[]{:S(2)}) copy-start(bf16[16,2,128,128]{3,2,1,0:T(8,128)(2,1)S(1)} %pad_maximum_fusion.sa) | copy-start | bytes 3145732
  35.3 1.1 %copy-start.4 = (bf16[8,2,128,128]{3,2,1,0:T(8,128)(2,1)}, bf16[8,2,128,128]{3,2,1,0:T(8,128)(2,1)S(1)}, u32[]{:S(2)}) copy-start(bf16[8,2,128,128]{3,2,1,0:T(8,128)(2,1)S(1)} %collective-permute-done.6.refs_5_) | copy-start | bytes 1572868
  35.4 14.7 %copy-start.1 = (bf16[16,2,128,128]{3,2,1,0:T(8,128)(2,1)}, bf16[16,2,128,128]{3,2,1,0:T(8,128)(2,1)S(1)}, u32[]{:S(2)}) copy-start(bf16[16,2,128,128]{3,2,1,0:T(8,128)(2,1)S(1)} %pad_maximum_fusion.1.sb) | copy-start | bytes 3145732
  35.4 15.2 %collective-permute-start.7 = (bf16[16,2,128,128]{3,2,1,0:T(8,128)(2,1)S(1)}, bf16[16,2,128,128]{3,2,1,0:T(8,128)(2,1)S(1)}, u32[]{:S(2)}, u32[]{:S(2)}) collective-permute-start(bf16[16,2,128,128]{3,2,1,0:T(8,128)(2,1)S(1)} %pad_maximum_fusion.sa), channel_id=1, source_target_pairs={{0,96},{1,13},{4,100},{5,9},{8,104},{9,5},{12,108},{13,1},{32,64},... | collective-permute-start | bytes 3145736 | tf_op jit(solution)/shard_map/ppermute | solution.py:340
  36.4 14.3 %collective-permute-start.8 = (bf16[16,2,128,128]{3,2,1,0:T(8,128)(2,1)S(1)}, bf16[16,2,128,128]{3,2,1,0:T(8,128)(2,1)}, u32[]{:S(2)}, u32[]{:S(2)}) collective-permute-start(bf16[16,2,128,128]{3,2,1,0:T(8,128)(2,1)S(1)} %pad_maximum_fusion.1.sb), channel_id=1, source_target_pairs={{0,32},{1,5},{4,36},{5,1},{8,40},{9,13},{12,44},{13,9},{32,0},{33,... | collective-permute-start | bytes 3145736 | tf_op jit(solution)/shard_map/ppermute | solution.py:340
  50.7 1.0 %copy-start.2 = (bf16[16,2,128,128]{3,2,1,0:T(8,128)(2,1)}, bf16[16,2,128,128]{3,2,1,0:T(8,128)(2,1)S(1)}, u32[]{:S(2)}) copy-start(bf16[16,2,128,128]{3,2,1,0:T(8,128)(2,1)S(1)} %collective-permute-done.7.refs_4_.ra) | copy-start | bytes 3145732
  53.9 21.6 %collective-permute-start.11 = (bf16[2,2,128,128]{3,2,1,0:T(8,128)(2,1)}, bf16[2,2,128,128]{3,2,1,0:T(8,128)(2,1)S(1)}, u32[]{:S(2)}, u32[]{:S(2)}) collective-permute-start(bf16[2,2,128,128]{3,2,1,0:T(8,128)(2,1)} %pick_pages.1.mine), channel_id=1, source_target_pairs={{0,3},{1,2},{2,1},{3,0},{4,7},{5,6},{6,5},{7,4},{8,11},{9,10},{10,... | collective-permute-start | bytes 393224 | tf_op jit(solution)/shard_map/ppermute | solution.py:384
  61.4 14.2 %collective-permute-start.10 = (bf16[2,2,128,128]{3,2,1,0:T(8,128)(2,1)}, bf16[2,2,128,128]{3,2,1,0:T(8,128)(2,1)S(1)}, u32[]{:S(2)}, u32[]{:S(2)}) collective-permute-start(bf16[2,2,128,128]{3,2,1,0:T(8,128)(2,1)} %pick_pages.1.mine), channel_id=1, source_target_pairs={{0,2},{1,3},{2,0},{3,1},{4,6},{5,7},{6,4},{7,5},{8,10},{9,11},{10,... | collective-permute-start | bytes 393224 | tf_op jit(solution)/shard_map/ppermute | solution.py:384
  61.4 14.2 %collective-permute-start.9 = (bf16[2,2,128,128]{3,2,1,0:T(8,128)(2,1)}, bf16[2,2,128,128]{3,2,1,0:T(8,128)(2,1)S(1)}, u32[]{:S(2)}, u32[]{:S(2)}) collective-permute-start(bf16[2,2,128,128]{3,2,1,0:T(8,128)(2,1)} %pick_pages.1.mine), channel_id=1, source_target_pairs={{0,1},{1,0},{2,3},{3,2},{4,5},{5,4},{6,7},{7,6},{8,9},{9,8},{10,11... | collective-permute-start | bytes 393224 | tf_op jit(solution)/shard_map/ppermute | solution.py:384
  75.5 0.6 copy-start.9
  75.5 0.7 copy-start.10
  76.2 0.7 copy-start.11

commit v3 on v2

--- a/solution.py
+++ b/solution.py
@@ -166,15 +166,14 @@
 
 
 def last_kernel(
-    table, q_ref, top_in, acc_in, b_ref, mine, core, zh, other, sa, sb, ra, rb,
-    out, pages, scales,
+    table, q_ref, top_in, acc_in, a_ref, b_ref, sa, sb, ra, rb,
+    out,
     top_ref, acc, hold, sems, worst, far_v, far,
 ):
     ins = ((top_in, top_ref), (acc_in, acc))
     for s in range(2):
         for k, (i, o) in enumerate(ins):
             pltpu.make_async_copy(i.at[s], o.at[s], sems.at[k, s]).start()
-    place(mine, core, zh, other, pages, scales)
     worst[...] = jnp.zeros_like(worst)
 
     def span(s, carry):
@@ -192,7 +191,8 @@
                 rows = pl.ds(pl.multiple_of(s * SP, SP), SP)
                 out[rows, head * DH : (head + 1) * DH] = done[h * SP : (h + 1) * SP]
 
-        span_sums(s, table, q_ref, ((b_ref, PIECES + PIECES // 2),), top_ref, store)
+        parts = ((a_ref, PIECES // 2), (b_ref, PIECES + PIECES // 2))
+        span_sums(s, table, q_ref, parts, top_ref, store)
         return carry
 
     lax.fori_loop(0, 2, span, 0)
@@ -383,12 +383,11 @@
     others = [
         lax.ppermute(mine, ("zh", "core"), [(i, i ^ away) for i in range(4)]) for away in (1, 2, 3)
     ]
-    acc = sums_of((16,), "attend_fourth", table, queries, top, acc, come[0])
-    attended, pages, scales = pl.pallas_call(
+    attended = pl.pallas_call(
         last_kernel,
-        out_shape=(bf16(2 * SP, HEADS * DH), bf16(2, 4, 2, SP, DH), f32(2, 2, 4)),
-        in_specs=[SM, VM] + [ANY] * 2 + [VM] * 5 + [ANY] * 4,
-        out_specs=(VM, VM, VM),
+        out_shape=bf16(2 * SP, HEADS * DH),
+        in_specs=[SM, VM] + [ANY] * 2 + [VM] * 2 + [ANY] * 4,
+        out_specs=VM,
         scratch_shapes=[
             pltpu.VMEM(TOPS, jnp.float32),
             pltpu.VMEM(SUMS, jnp.float32),
@@ -399,11 +398,15 @@
             pltpu.SemaphoreType.DMA((4,)),
         ],
         name="attend_last",
-        **options(16),
-    )(
-        table, queries, top, acc, come[1], mine, *others,
-        held[0], held[1], come[0], come[1],
-    )
+        **options(32),
+    )(table, queries, top, acc, come[0], come[1], held[0], held[1], come[0], come[1])
+    pages, scales = pl.pallas_call(
+        place,
+        out_shape=(bf16(2, 4, 2, SP, DH), f32(2, 2, 4)),
+        in_specs=[VM] * 4,
+        out_specs=(VM, VM),
+        name="place_pages",
+    )(mine, *others)
     return attended, pages, scales.transpose(0, 2, 1)
 
 

time: 91.7 us -> 88.8 us (0.968)
  Pallas kernels: 60.3 us -> 57.5 us
    pallas_call x3 -> x2, Pallas kernels: 36.4 us -> 22.8 us  [sums_of(): pl.pallas_call(lambda *refs: next_kernel(firsts, *refs), out_shape=f32(*S...]
    pallas_call x1 -> x2, Pallas kernels: 14.3 us -> 25.1 us  [the longest x1 23 us: on_device(): pl.pallas_call(last_kernel, out_shape=bf16(2 * SP, HEADS * DH), in_specs=...]
  transfers between devices with their start and end apart: 12 -> 12, of which waited for: 4 -> 4; matrix products, arithmetic and copies ran while one was open for 2% -> 2% of each run, Pallas kernels for 48% -> 60%
where the time goes in v3:
time: 88.8 us; the launch traced here: 88.4 us
  Pallas kernels  57.5 us (65%)
  starting transfers between devices  18.3 us (21%)
  waiting for transfers between devices  6.35 us (7%)
  other arithmetic  2.9 us (3%)
  local copies, waits for them, and re-layouts  2.33 us (3%)
  between operations  0.91 us (1%)
    pallas_call x1, Pallas kernels, on_device(): pl.pallas_call(last_kernel, out_shape=bf16(2 * SP, HEADS * DH), in_specs=...  23 us
    pallas_call x2, Pallas kernels, sums_of(): pl.pallas_call(lambda *refs: next_kernel(firsts, *refs), out_shape=f32(*S...  22.8 us
    ppermute x3, starting transfers between devices, on_device(): lax.ppermute(mine, ('zh', 'core'), [(i, i ^ away) for i in range(4)])  7.98 us
    ppermute x8, starting transfers between devices, swap(): return lax.ppermute(x, ('y', 'x', 'core'), pairs)  7.82 us
    pallas_call x1, Pallas kernels, on_device(): pl.pallas_call(first_kernel, out_shape=(f32(*TOPS), f32(*SUMS)), in_specs...  7.45 us
    ppermute x8, waiting for transfers between devices, swap(): return lax.ppermute(x, ('y', 'x', 'core'), pairs)  4.02 us
    ppermute x1, starting transfers between devices, on_device(): lax.ppermute(own, 'zl', [(0, 1), (1, 0)])  2.55 us
    unnamed x24, local copies, waits for them, and re-layouts  2.33 us
  transfers between devices with their start and end apart: 12, of which 4 were waited for; matrix products, arithmetic and copies ran while one was open for 2% of the time, Pallas kernels for 60%

profile of v3, /device:TPU:1, one launch (start us, length us, event | category | flops | bytes accessed | tf_op | source)
XLA Modules:
  0.0 88.4 jit_solution(1454767533753914692)
XLA Ops:
  0.6 0.9 %maximum_bitcast_fusion = bf16[2,1,2,128,128]{4,3,2,1,0:T(8,128)(2,1)S(1)} fusion(bf16[2,1,128,128]{3,2,1,0:T(8,128)(2,1)} %bitcast.9, bf16[2,1,128,128]{3,2,1,0:T(8,128)(2,1)} %bitcast.10), kind=kLoop, calls=%fused_computation.12 | loop fusion | flops 65536 | bytes 262144 | tf_op jit(solution)/shard_map/broadcast_in_dim | solution.py:344
  1.5 2.5 %collective-permute-start = (bf16[2,1,2,128,128]{4,3,2,1,0:T(8,128)(2,1)S(1)}, bf16[2,1,2,128,128]{4,3,2,1,0:T(8,128)(2,1)S(1)}, u32[]{:S(2)}, u32[]{:S(2)}) collective-permute-start(bf16[2,1,2,128,128]{4,3,2,1,0:T(8,128)(2,1)S(1)} %maximum_bitcast_fusion), channel_id=1, source_target_pairs={{0,16},{16,0},{1,17},{17,1},{2,18},{18,2},{3,19},{19,3},{4,20},{20... | collective-permute-start | bytes 393224 | tf_op jit(solution)/shard_map/ppermute | solution.py:345
  4.1 0.8 select_reduce_fusion.1
  5.0 2.3 %collective-permute-done = bf16[2,1,2,128,128]{4,3,2,1,0:T(8,128)(2,1)S(1)} collective-permute-done((bf16[2,1,2,128,128]{4,3,2,1,0:T(8,128)(2,1)S(1)}, bf16[2,1,2,128,128]{4,3,2,1,0:T(8,128)(2,1)S(1)}, u32[]{:S(2)}, u32[]{:S(2)}) %collective-permute-start) | collective-permute-done | bytes 131104 | tf_op jit(solution)/shard_map/ppermute | solution.py:345
  7.3 2.7 %collective-permute-start.2 = (bf16[2,2,128,128]{3,2,1,0:T(8,128)(2,1)S(1)}, bf16[2,2,128,128]{3,2,1,0:T(8,128)(2,1)S(1)}, u32[]{:S(2)}, u32[]{:S(2)}) collective-permute-start(bf16[2,2,128,128]{3,2,1,0:T(8,128)(2,1)S(1)} %get-tuple-element.25), channel_id=1, source_target_pairs={{0,12},{1,97},{4,8},{5,101},{8,4},{9,105},{12,0},{13,109},{32,44},... | collective-permute-start | bytes 393224 | tf_op jit(solution)/shard_map/ppermute | solution.py:340
  10.0 0.2 fusion.3
  10.2 0.1 collective-permute-start.1
  10.3 0.6 pad_add_fusion.table.refs_0_
  10.9 1.5 %collective-permute-done.2 = bf16[2,2,128,128]{3,2,1,0:T(8,128)(2,1)S(1)} collective-permute-done((bf16[2,2,128,128]{3,2,1,0:T(8,128)(2,1)S(1)}, bf16[2,2,128,128]{3,2,1,0:T(8,128)(2,1)S(1)}, u32[]{:S(2)}, u32[]{:S(2)}) %collective-permute-start.2) | collective-permute-done | bytes 131104 | tf_op jit(solution)/shard_map/ppermute | solution.py:340
  12.4 0.1 collective-permute-start.4
  12.5 1.8 %collective-permute-done.1 = bf16[2,2,128,128]{3,2,1,0:T(8,128)(2,1)S(1)} collective-permute-done((bf16[2,2,128,128]{3,2,1,0:T(8,128)(2,1)S(1)}, bf16[2,2,128,128]{3,2,1,0:T(8,128)(2,1)S(1)}, u32[]{:S(2)}, u32[]{:S(2)}) %collective-permute-start.1) | collective-permute-done | bytes 131104 | tf_op jit(solution)/shard_map/ppermute | solution.py:340
  14.4 0.9 %collective-permute-start.3 = (bf16[4,2,128,128]{3,2,1,0:T(8,128)(2,1)S(1)}, bf16[4,2,128,128]{3,2,1,0:T(8,128)(2,1)S(1)}, u32[]{:S(2)}, u32[]{:S(2)}) collective-permute-start(bf16[4,2,128,128]{3,2,1,0:T(8,128)(2,1)S(1)} %pad_maximum_fusion.4.a_ref), channel_id=1, source_target_pairs={{0,12},{1,97},{4,8},{5,101},{8,4},{9,105},{12,0},{13,109},{32,44},... | collective-permute-start | bytes 786440 | tf_op jit(solution)/shard_map/ppermute | solution.py:340
  15.3 7.5 %attend_first.1 = (f32[2,2048,128]{2,1,0:T(8,128)}, f32[2,2048,256]{2,1,0:T(8,128)}) custom-call(s32[66]{0:T(128)} %pad_add_fusion.table.refs_0_, bf16[256,2048]{1,0:T(8,128)(2,1)} %q_ref.3, bf16[4,2,128,128]{3,2,1,0:T(8,128)(2,1)} %copy-done.6, bf16[4,2,128,128]{3,2,1,0:T(8,128)(2,1)} %copy-done.5), custom_call_target="tpu_custom_call" | custom-call | flops 4294967296 | bytes 8388608 | tf_op jit(solution)/shard_map/attend_first/pallas_call | solution.py:357
  22.8 0.1 pad_maximum_fusion.3
  22.9 0.1 pad_maximum_fusion.2
  23.0 1.3 %collective-permute-start.5 = (bf16[8,2,128,128]{3,2,1,0:T(8,128)(2,1)S(1)}, bf16[8,2,128,128]{3,2,1,0:T(8,128)(2,1)S(1)}, u32[]{:S(2)}, u32[]{:S(2)}) collective-permute-start(bf16[8,2,128,128]{3,2,1,0:T(8,128)(2,1)S(1)} %pad_maximum_fusion.2), channel_id=1, source_target_pairs={{0,32},{1,5},{4,36},{5,1},{8,40},{9,13},{12,44},{13,9},{32,0},{33,... | collective-permute-start | bytes 1572872 | tf_op jit(solution)/shard_map/ppermute | solution.py:340
  24.2 1.8 %collective-permute-start.6 = (bf16[8,2,128,128]{3,2,1,0:T(8,128)(2,1)S(1)}, bf16[8,2,128,128]{3,2,1,0:T(8,128)(2,1)S(1)}, u32[]{:S(2)}, u32[]{:S(2)}) collective-permute-start(bf16[8,2,128,128]{3,2,1,0:T(8,128)(2,1)S(1)} %pad_maximum_fusion.3), channel_id=1, source_target_pairs={{0,96},{1,13},{4,100},{5,9},{8,104},{9,5},{12,108},{13,1},{32,64},... | collective-permute-start | bytes 1572872 | tf_op jit(solution)/shard_map/ppermute | solution.py:340
  26.1 9.1 %attend_second.1.refs_3_ = f32[2,2048,256]{2,1,0:T(8,128)} custom-call(s32[66]{0:T(128)} %pad_add_fusion.table.refs_0_, bf16[256,2048]{1,0:T(8,128)(2,1)} %q_ref.3, f32[2,2048,128]{2,1,0:T(8,128)} %get-tuple-element.13.refs_2_.top_in, f32[2,2048,256]{2,1,0:T(8,128)} %get-tuple-element.17.refs_3_, bf16[4,2,128,128]{3,2,1,0:T(8,128)(2,1)} %copy-done.8, ...), custom_call_target="tpu_custom_call" | custom-call | flops 4294967296 | bytes 8388608 | tf_op jit(solution)/shard_map/attend_second/pallas_call | solution.py:321
  35.2 0.1 pad_maximum_fusion.sa
  35.4 0.1 pad_maximum_fusion.1.sb
  35.5 0.9 %collective-permute-start.7 = (bf16[16,2,128,128]{3,2,1,0:T(8,128)(2,1)S(1)}, bf16[16,2,128,128]{3,2,1,0:T(8,128)(2,1)S(1)}, u32[]{:S(2)}, u32[]{:S(2)}) collective-permute-start(bf16[16,2,128,128]{3,2,1,0:T(8,128)(2,1)S(1)} %pad_maximum_fusion.sa), channel_id=1, source_target_pairs={{0,96},{1,13},{4,100},{5,9},{8,104},{9,5},{12,108},{13,1},{32,64},... | collective-permute-start | bytes 3145736 | tf_op jit(solution)/shard_map/ppermute | solution.py:340
  36.4 13.6 %attend_third.1.acc_in = f32[2,2048,256]{2,1,0:T(8,128)} custom-call(s32[66]{0:T(128)} %pad_add_fusion.table.refs_0_, bf16[256,2048]{1,0:T(8,128)(2,1)} %q_ref.3, f32[2,2048,128]{2,1,0:T(8,128)} %get-tuple-element.13.refs_2_.top_in, f32[2,2048,256]{2,1,0:T(8,128)} %attend_second.1.refs_3_, bf16[8,2,128,128]{3,2,1,0:T(8,128)(2,1)} %copy-done.3, ...), custom_call_target="tpu_custom_call" | custom-call | flops 8589934592 | bytes 8388608 | tf_op jit(solution)/shard_map/attend_third/pallas_call | solution.py:321
  50.1 0.6 collective-permute-done.7.a_ref.ra
  50.7 1.0 %copy-done.2 = bf16[16,2,128,128]{3,2,1,0:T(8,128)(2,1)} copy-done((bf16[16,2,128,128]{3,2,1,0:T(8,128)(2,1)}, bf16[16,2,128,128]{3,2,1,0:T(8,128)(2,1)S(1)}, u32[]{:S(2)}) %copy-start.2) | copy-done | bytes 1048600
  51.7 2.2 %pick_pages.1.mine = bf16[2,2,128,128]{3,2,1,0:T(8,128)(2,1)} custom-call(s32[66]{0:T(128)} %pad_add_fusion.table.refs_0_, bf16[16,2,128,128]{3,2,1,0:T(8,128)(2,1)} %copy-done, bf16[16,2,128,128]{3,2,1,0:T(8,128)(2,1)} %copy-done.2, bf16[16,2,128,128]{3,2,1,0:T(8,128)(2,1)} %copy-done.1, bf16[16,2,128,128]{3,2,1,0:T(8,128)(2,1)} %collective-permute-done.8.b_ref.rb), custom_call_target="tpu_custom_call" | custom-call | tf_op jit(solution)/shard_map/pick_pages/pallas_call | solution.py:375
  53.9 7.5 %collective-permute-start.11 = (bf16[2,2,128,128]{3,2,1,0:T(8,128)(2,1)}, bf16[2,2,128,128]{3,2,1,0:T(8,128)(2,1)S(1)}, u32[]{:S(2)}, u32[]{:S(2)}) collective-permute-start(bf16[2,2,128,128]{3,2,1,0:T(8,128)(2,1)} %pick_pages.1.mine), channel_id=1, source_target_pairs={{0,3},{1,2},{2,1},{3,0},{4,7},{5,6},{6,5},{7,4},{8,11},{9,10},{10,... | collective-permute-start | bytes 393224 | tf_op jit(solution)/shard_map/ppermute | solution.py:384
  61.4 0.5 collective-permute-start.9
  61.9 23.0 %attend_last.1 = bf16[256,2048]{1,0:T(8,128)(2,1)} custom-call(s32[66]{0:T(128)} %pad_add_fusion.table.refs_0_, bf16[256,2048]{1,0:T(8,128)(2,1)} %q_ref.3, f32[2,2048,128]{2,1,0:T(8,128)} %get-tuple-element.13.refs_2_.top_in, f32[2,2048,256]{2,1,0:T(8,128)} %attend_third.1.acc_in, bf16[16,2,128,128]{3,2,1,0:T(8,128)(2,1)} %copy-done.2, ...), custom_call_target="tpu_custom_call" | custom-call | flops 17179869184 | bytes 8388608 | tf_op jit(solution)/shard_map/attend_last/pallas_call | solution.py:386
  85.0 0.6 copy-done.9
  85.6 0.1 copy-done.10
  85.6 0.7 copy-done.11
  86.3 2.1 %place_pages.1 = (bf16[2,4,2,128,128]{4,3,2,1,0:T(8,128)(2,1)}, f32[2,2,4]{2,1,0:T(2,128)}) custom-call(bf16[2,2,128,128]{3,2,1,0:T(8,128)(2,1)} %pick_pages.1.mine, bf16[2,2,128,128]{3,2,1,0:T(8,128)(2,1)} %copy-done.11, bf16[2,2,128,128]{3,2,1,0:T(8,128)(2,1)} %copy-done.10, bf16[2,2,128,128]{3,2,1,0:T(8,128)(2,1)} %copy-done.9), custom_call_target="tpu_custom_call" | custom-call | tf_op jit(solution)/shard_map/place_pages/pallas_call | solution.py:403
  (35 shorter events, 0.2 us)
Async XLA Ops:
  1.5 5.7 %collective-permute-start = (bf16[2,1,2,128,128]{4,3,2,1,0:T(8,128)(2,1)S(1)}, bf16[2,1,2,128,128]{4,3,2,1,0:T(8,128)(2,1)S(1)}, u32[]{:S(2)}, u32[]{:S(2)}) collective-permute-start(bf16[2,1,2,128,128]{4,3,2,1,0:T(8,128)(2,1)S(1)} %maximum_bitcast_fusion), channel_id=1, source_target_pairs={{0,16},{16,0},{1,17},{17,1},{2,18},{18,2},{3,19},{19,3},{4,20},{20... | collective-permute-start | bytes 393224 | tf_op jit(solution)/shard_map/ppermute | solution.py:345
  7.3 5.1 %collective-permute-start.2 = (bf16[2,2,128,128]{3,2,1,0:T(8,128)(2,1)S(1)}, bf16[2,2,128,128]{3,2,1,0:T(8,128)(2,1)S(1)}, u32[]{:S(2)}, u32[]{:S(2)}) collective-permute-start(bf16[2,2,128,128]{3,2,1,0:T(8,128)(2,1)S(1)} %get-tuple-element.25), channel_id=1, source_target_pairs={{0,12},{1,97},{4,8},{5,101},{8,4},{9,105},{12,0},{13,109},{32,44},... | collective-permute-start | bytes 393224 | tf_op jit(solution)/shard_map/ppermute | solution.py:340
  10.2 4.2 %collective-permute-start.1 = (bf16[2,2,128,128]{3,2,1,0:T(8,128)(2,1)S(1)}, bf16[2,2,128,128]{3,2,1,0:T(8,128)(2,1)S(1)}, u32[]{:S(2)}, u32[]{:S(2)}) collective-permute-start(bf16[2,2,128,128]{3,2,1,0:T(8,128)(2,1)S(1)} %get-tuple-element.26), channel_id=1, source_target_pairs={{0,4},{1,33},{4,0},{5,37},{8,12},{9,41},{12,8},{13,45},{32,36},{33... | collective-permute-start | bytes 393224 | tf_op jit(solution)/shard_map/ppermute | solution.py:340
  12.4 2.9 %copy-start.5 = (bf16[4,2,128,128]{3,2,1,0:T(8,128)(2,1)}, bf16[4,2,128,128]{3,2,1,0:T(8,128)(2,1)S(1)}, u32[]{:S(2)}) copy-start(bf16[4,2,128,128]{3,2,1,0:T(8,128)(2,1)S(1)} %pad_maximum_fusion.5.b_ref) | copy-start | bytes 786436
  12.4 10.3 %collective-permute-start.4 = (bf16[4,2,128,128]{3,2,1,0:T(8,128)(2,1)S(1)}, bf16[4,2,128,128]{3,2,1,0:T(8,128)(2,1)S(1)}, u32[]{:S(2)}, u32[]{:S(2)}) collective-permute-start(bf16[4,2,128,128]{3,2,1,0:T(8,128)(2,1)S(1)} %pad_maximum_fusion.5.b_ref), channel_id=1, source_target_pairs={{0,4},{1,33},{4,0},{5,37},{8,12},{9,41},{12,8},{13,45},{32,36},{33... | collective-permute-start | bytes 786440 | tf_op jit(solution)/shard_map/ppermute | solution.py:340
  14.4 0.9 %copy-start.6 = (bf16[4,2,128,128]{3,2,1,0:T(8,128)(2,1)}, bf16[4,2,128,128]{3,2,1,0:T(8,128)(2,1)S(1)}, u32[]{:S(2)}) copy-start(bf16[4,2,128,128]{3,2,1,0:T(8,128)(2,1)S(1)} %pad_maximum_fusion.4.a_ref) | copy-start | bytes 786436
  14.4 8.4 %collective-permute-start.3 = (bf16[4,2,128,128]{3,2,1,0:T(8,128)(2,1)S(1)}, bf16[4,2,128,128]{3,2,1,0:T(8,128)(2,1)S(1)}, u32[]{:S(2)}, u32[]{:S(2)}) collective-permute-start(bf16[4,2,128,128]{3,2,1,0:T(8,128)(2,1)S(1)} %pad_maximum_fusion.4.a_ref), channel_id=1, source_target_pairs={{0,12},{1,97},{4,8},{5,101},{8,4},{9,105},{12,0},{13,109},{32,44},... | collective-permute-start | bytes 786440 | tf_op jit(solution)/shard_map/ppermute | solution.py:340
  22.8 3.3 %copy-start.7 = (bf16[4,2,128,128]{3,2,1,0:T(8,128)(2,1)}, bf16[4,2,128,128]{3,2,1,0:T(8,128)(2,1)S(1)}, u32[]{:S(2)}) copy-start(bf16[4,2,128,128]{3,2,1,0:T(8,128)(2,1)S(1)} %collective-permute-done.4.refs_5_) | copy-start | bytes 786436
  22.9 3.2 %copy-start.8 = (bf16[4,2,128,128]{3,2,1,0:T(8,128)(2,1)}, bf16[4,2,128,128]{3,2,1,0:T(8,128)(2,1)S(1)}, u32[]{:S(2)}) copy-start(bf16[4,2,128,128]{3,2,1,0:T(8,128)(2,1)S(1)} %collective-permute-done.3.refs_4_) | copy-start | bytes 786436
  23.0 12.2 %collective-permute-start.5 = (bf16[8,2,128,128]{3,2,1,0:T(8,128)(2,1)S(1)}, bf16[8,2,128,128]{3,2,1,0:T(8,128)(2,1)S(1)}, u32[]{:S(2)}, u32[]{:S(2)}) collective-permute-start(bf16[8,2,128,128]{3,2,1,0:T(8,128)(2,1)S(1)} %pad_maximum_fusion.2), channel_id=1, source_target_pairs={{0,32},{1,5},{4,36},{5,1},{8,40},{9,13},{12,44},{13,9},{32,0},{33,... | collective-permute-start | bytes 1572872 | tf_op jit(solution)/shard_map/ppermute | solution.py:340
  24.2 11.1 %collective-permute-start.6 = (bf16[8,2,128,128]{3,2,1,0:T(8,128)(2,1)S(1)}, bf16[8,2,128,128]{3,2,1,0:T(8,128)(2,1)S(1)}, u32[]{:S(2)}, u32[]{:S(2)}) collective-permute-start(bf16[8,2,128,128]{3,2,1,0:T(8,128)(2,1)S(1)} %pad_maximum_fusion.3), channel_id=1, source_target_pairs={{0,96},{1,13},{4,100},{5,9},{8,104},{9,5},{12,108},{13,1},{32,64},... | collective-permute-start | bytes 1572872 | tf_op jit(solution)/shard_map/ppermute | solution.py:340
  35.2 1.2 %copy-start.3 = (bf16[8,2,128,128]{3,2,1,0:T(8,128)(2,1)}, bf16[8,2,128,128]{3,2,1,0:T(8,128)(2,1)S(1)}, u32[]{:S(2)}) copy-start(bf16[8,2,128,128]{3,2,1,0:T(8,128)(2,1)S(1)} %collective-permute-done.5.refs_4_) | copy-start | bytes 1572868
  35.3 14.7 %copy-start = (bf16[16,2,128,128]{3,2,1,0:T(8,128)(2,1)}, bf16[16,2,128,128]{3,2,1,0:T(8,128)(2,1)S(1)}, u32[]{:S(2)}) copy-start(bf16[16,2,128,128]{3,2,1,0:T(8,128)(2,1)S(1)} %pad_maximum_fusion.sa) | copy-start | bytes 3145732
  35.3 1.1 %copy-start.4 = (bf16[8,2,128,128]{3,2,1,0:T(8,128)(2,1)}, bf16[8,2,128,128]{3,2,1,0:T(8,128)(2,1)S(1)}, u32[]{:S(2)}) copy-start(bf16[8,2,128,128]{3,2,1,0:T(8,128)(2,1)S(1)} %collective-permute-done.6.refs_5_) | copy-start | bytes 1572868
  35.5 14.6 %copy-start.1 = (bf16[16,2,128,128]{3,2,1,0:T(8,128)(2,1)}, bf16[16,2,128,128]{3,2,1,0:T(8,128)(2,1)S(1)}, u32[]{:S(2)}) copy-start(bf16[16,2,128,128]{3,2,1,0:T(8,128)(2,1)S(1)} %pad_maximum_fusion.1.sb) | copy-start | bytes 3145732
  35.5 15.2 %collective-permute-start.7 = (bf16[16,2,128,128]{3,2,1,0:T(8,128)(2,1)S(1)}, bf16[16,2,128,128]{3,2,1,0:T(8,128)(2,1)S(1)}, u32[]{:S(2)}, u32[]{:S(2)}) collective-permute-start(bf16[16,2,128,128]{3,2,1,0:T(8,128)(2,1)S(1)} %pad_maximum_fusion.sa), channel_id=1, source_target_pairs={{0,96},{1,13},{4,100},{5,9},{8,104},{9,5},{12,108},{13,1},{32,64},... | collective-permute-start | bytes 3145736 | tf_op jit(solution)/shard_map/ppermute | solution.py:340
  36.4 14.3 %collective-permute-start.8 = (bf16[16,2,128,128]{3,2,1,0:T(8,128)(2,1)S(1)}, bf16[16,2,128,128]{3,2,1,0:T(8,128)(2,1)}, u32[]{:S(2)}, u32[]{:S(2)}) collective-permute-start(bf16[16,2,128,128]{3,2,1,0:T(8,128)(2,1)S(1)} %pad_maximum_fusion.1.sb), channel_id=1, source_target_pairs={{0,32},{1,5},{4,36},{5,1},{8,40},{9,13},{12,44},{13,9},{32,0},{33,... | collective-permute-start | bytes 3145736 | tf_op jit(solution)/shard_map/ppermute | solution.py:340
  50.7 1.0 %copy-start.2 = (bf16[16,2,128,128]{3,2,1,0:T(8,128)(2,1)}, bf16[16,2,128,128]{3,2,1,0:T(8,128)(2,1)S(1)}, u32[]{:S(2)}) copy-start(bf16[16,2,128,128]{3,2,1,0:T(8,128)(2,1)S(1)} %collective-permute-done.7.a_ref.ra) | copy-start | bytes 3145732
  53.9 31.0 %collective-permute-start.11 = (bf16[2,2,128,128]{3,2,1,0:T(8,128)(2,1)}, bf16[2,2,128,128]{3,2,1,0:T(8,128)(2,1)S(1)}, u32[]{:S(2)}, u32[]{:S(2)}) collective-permute-start(bf16[2,2,128,128]{3,2,1,0:T(8,128)(2,1)} %pick_pages.1.mine), channel_id=1, source_target_pairs={{0,3},{1,2},{2,1},{3,0},{4,7},{5,6},{6,5},{7,4},{8,11},{9,10},{10,... | collective-permute-start | bytes 393224 | tf_op jit(solution)/shard_map/ppermute | solution.py:384
  61.4 23.5 %collective-permute-start.10 = (bf16[2,2,128,128]{3,2,1,0:T(8,128)(2,1)}, bf16[2,2,128,128]{3,2,1,0:T(8,128)(2,1)S(1)}, u32[]{:S(2)}, u32[]{:S(2)}) collective-permute-start(bf16[2,2,128,128]{3,2,1,0:T(8,128)(2,1)} %pick_pages.1.mine), channel_id=1, source_target_pairs={{0,2},{1,3},{2,0},{3,1},{4,6},{5,7},{6,4},{7,5},{8,10},{9,11},{10,... | collective-permute-start | bytes 393224 | tf_op jit(solution)/shard_map/ppermute | solution.py:384
  61.4 23.6 %collective-permute-start.9 = (bf16[2,2,128,128]{3,2,1,0:T(8,128)(2,1)}, bf16[2,2,128,128]{3,2,1,0:T(8,128)(2,1)S(1)}, u32[]{:S(2)}, u32[]{:S(2)}) collective-permute-start(bf16[2,2,128,128]{3,2,1,0:T(8,128)(2,1)} %pick_pages.1.mine), channel_id=1, source_target_pairs={{0,1},{1,0},{2,3},{3,2},{4,5},{5,4},{6,7},{7,6},{8,9},{9,8},{10,11... | collective-permute-start | bytes 393224 | tf_op jit(solution)/shard_map/ppermute | solution.py:384
  84.9 0.6 copy-start.9
  84.9 0.7 copy-start.10
  85.6 0.7 copy-start.11

commit v4 on v3

--- a/solution.py
+++ b/solution.py
@@ -167,8 +167,8 @@
 
 def last_kernel(
     table, q_ref, top_in, acc_in, a_ref, b_ref, sa, sb, ra, rb,
-    out,
-    top_ref, acc, hold, sems, worst, far_v, far,
+    result,
+    top_ref, acc, hold, sems, worst, far_v, far, out, leave,
 ):
     ins = ((top_in, top_ref), (acc_in, acc))
     for s in range(2):
@@ -193,9 +193,14 @@
 
         parts = ((a_ref, PIECES // 2), (b_ref, PIECES + PIECES // 2))
         span_sums(s, table, q_ref, parts, top_ref, store)
+        mine = pl.ds(pl.multiple_of(s * SP, SP), SP)
+        pltpu.make_async_copy(out.at[mine], result.at[mine], leave.at[s]).start()
         return carry
 
     lax.fori_loop(0, 2, span, 0)
+    for s in range(2):
+        mine = pl.ds(s * SP, SP)
+        pltpu.make_async_copy(out.at[mine], result.at[mine], leave.at[s]).wait()
 
     @pl.when(jnp.max(worst[...]) > 0.0)
     def _():
@@ -209,6 +214,9 @@
         for copy in fetch:
             copy.wait()
         rescaled(table, q_ref, far_v, out, acc.at[0], hold)
+        again = pltpu.make_async_copy(out, result, leave.at[0])
+        again.start()
+        again.wait()
 
 
 def rescaled(table, q_ref, held, out, acc, hold):
@@ -387,7 +395,7 @@
         last_kernel,
         out_shape=bf16(2 * SP, HEADS * DH),
         in_specs=[SM, VM] + [ANY] * 2 + [VM] * 2 + [ANY] * 4,
-        out_specs=VM,
+        out_specs=ANY,
         scratch_shapes=[
             pltpu.VMEM(TOPS, jnp.float32),
             pltpu.VMEM(SUMS, jnp.float32),
@@ -396,6 +404,8 @@
             pltpu.VMEM((TILE * SP, DH), jnp.float32),
             pltpu.VMEM((2 * PIECES, 2, SP, DH), jnp.bfloat16),
             pltpu.SemaphoreType.DMA((4,)),
+            pltpu.VMEM((2 * SP, HEADS * DH), jnp.bfloat16),
+            pltpu.SemaphoreType.DMA((2,)),
         ],
         name="attend_last",
         **options(32),

time: 88.8 us -> 88.6 us (level)
  no operation moved by 1% of the time
where the time goes in v4:
time: 88.6 us; the launch traced here: 88.2 us
  Pallas kernels  57.4 us (65%)
  starting transfers between devices  18.3 us (21%)
  waiting for transfers between devices  6.35 us (7%)
  other arithmetic  2.9 us (3%)
  local copies, waits for them, and re-layouts  2.33 us (3%)
  between operations  0.91 us (1%)
    pallas_call x1, Pallas kernels, on_device(): pl.pallas_call(last_kernel, out_shape=bf16(2 * SP, HEADS * DH), in_specs=...  22.9 us
    pallas_call x2, Pallas kernels, sums_of(): pl.pallas_call(lambda *refs: next_kernel(firsts, *refs), out_shape=f32(*S...  22.8 us
    ppermute x3, starting transfers between devices, on_device(): lax.ppermute(mine, ('zh', 'core'), [(i, i ^ away) for i in range(4)])  7.98 us
    ppermute x8, starting transfers between devices, swap(): return lax.ppermute(x, ('y', 'x', 'core'), pairs)  7.82 us
    pallas_call x1, Pallas kernels, on_device(): pl.pallas_call(first_kernel, out_shape=(f32(*TOPS), f32(*SUMS)), in_specs...  7.45 us
    ppermute x8, waiting for transfers between devices, swap(): return lax.ppermute(x, ('y', 'x', 'core'), pairs)  4.02 us
    ppermute x1, starting transfers between devices, on_device(): lax.ppermute(own, 'zl', [(0, 1), (1, 0)])  2.55 us
    unnamed x24, local copies, waits for them, and re-layouts  2.33 us
  transfers between devices with their start and end apart: 12, of which 4 were waited for; matrix products, arithmetic and copies ran while one was open for 2% of the time, Pallas kernels for 60%

profile of v4, /device:TPU:1, one launch (start us, length us, event | category | flops | bytes accessed | tf_op | source)
XLA Modules:
  0.0 88.2 jit_solution(9126024954484291022)
XLA Ops:
  0.6 0.9 %maximum_bitcast_fusion = bf16[2,1,2,128,128]{4,3,2,1,0:T(8,128)(2,1)S(1)} fusion(bf16[2,1,128,128]{3,2,1,0:T(8,128)(2,1)} %bitcast.9, bf16[2,1,128,128]{3,2,1,0:T(8,128)(2,1)} %bitcast.10), kind=kLoop, calls=%fused_computation.12 | loop fusion | flops 65536 | bytes 262144 | tf_op jit(solution)/shard_map/broadcast_in_dim | solution.py:352
  1.5 2.5 %collective-permute-start = (bf16[2,1,2,128,128]{4,3,2,1,0:T(8,128)(2,1)S(1)}, bf16[2,1,2,128,128]{4,3,2,1,0:T(8,128)(2,1)S(1)}, u32[]{:S(2)}, u32[]{:S(2)}) collective-permute-start(bf16[2,1,2,128,128]{4,3,2,1,0:T(8,128)(2,1)S(1)} %maximum_bitcast_fusion), channel_id=1, source_target_pairs={{0,16},{16,0},{1,17},{17,1},{2,18},{18,2},{3,19},{19,3},{4,20},{20... | collective-permute-start | bytes 393224 | tf_op jit(solution)/shard_map/ppermute | solution.py:353
  4.1 0.8 select_reduce_fusion.1
  5.0 2.3 %collective-permute-done = bf16[2,1,2,128,128]{4,3,2,1,0:T(8,128)(2,1)S(1)} collective-permute-done((bf16[2,1,2,128,128]{4,3,2,1,0:T(8,128)(2,1)S(1)}, bf16[2,1,2,128,128]{4,3,2,1,0:T(8,128)(2,1)S(1)}, u32[]{:S(2)}, u32[]{:S(2)}) %collective-permute-start) | collective-permute-done | bytes 131104 | tf_op jit(solution)/shard_map/ppermute | solution.py:353
  7.3 2.7 %collective-permute-start.2 = (bf16[2,2,128,128]{3,2,1,0:T(8,128)(2,1)S(1)}, bf16[2,2,128,128]{3,2,1,0:T(8,128)(2,1)S(1)}, u32[]{:S(2)}, u32[]{:S(2)}) collective-permute-start(bf16[2,2,128,128]{3,2,1,0:T(8,128)(2,1)S(1)} %get-tuple-element.25), channel_id=1, source_target_pairs={{0,12},{1,97},{4,8},{5,101},{8,4},{9,105},{12,0},{13,109},{32,44},... | collective-permute-start | bytes 393224 | tf_op jit(solution)/shard_map/ppermute | solution.py:348
  10.0 0.2 fusion.3
  10.2 0.1 collective-permute-start.1
  10.3 0.6 pad_add_fusion.table.refs_0_
  10.9 1.5 %collective-permute-done.2 = bf16[2,2,128,128]{3,2,1,0:T(8,128)(2,1)S(1)} collective-permute-done((bf16[2,2,128,128]{3,2,1,0:T(8,128)(2,1)S(1)}, bf16[2,2,128,128]{3,2,1,0:T(8,128)(2,1)S(1)}, u32[]{:S(2)}, u32[]{:S(2)}) %collective-permute-start.2) | collective-permute-done | bytes 131104 | tf_op jit(solution)/shard_map/ppermute | solution.py:348
  12.4 0.1 collective-permute-start.4
  12.5 1.8 %collective-permute-done.1 = bf16[2,2,128,128]{3,2,1,0:T(8,128)(2,1)S(1)} collective-permute-done((bf16[2,2,128,128]{3,2,1,0:T(8,128)(2,1)S(1)}, bf16[2,2,128,128]{3,2,1,0:T(8,128)(2,1)S(1)}, u32[]{:S(2)}, u32[]{:S(2)}) %collective-permute-start.1) | collective-permute-done | bytes 131104 | tf_op jit(solution)/shard_map/ppermute | solution.py:348
  14.4 0.9 %collective-permute-start.3 = (bf16[4,2,128,128]{3,2,1,0:T(8,128)(2,1)S(1)}, bf16[4,2,128,128]{3,2,1,0:T(8,128)(2,1)S(1)}, u32[]{:S(2)}, u32[]{:S(2)}) collective-permute-start(bf16[4,2,128,128]{3,2,1,0:T(8,128)(2,1)S(1)} %pad_maximum_fusion.4.a_ref), channel_id=1, source_target_pairs={{0,12},{1,97},{4,8},{5,101},{8,4},{9,105},{12,0},{13,109},{32,44},... | collective-permute-start | bytes 786440 | tf_op jit(solution)/shard_map/ppermute | solution.py:348
  15.3 7.5 %attend_first.1 = (f32[2,2048,128]{2,1,0:T(8,128)}, f32[2,2048,256]{2,1,0:T(8,128)}) custom-call(s32[66]{0:T(128)} %pad_add_fusion.table.refs_0_, bf16[256,2048]{1,0:T(8,128)(2,1)} %q_ref.3, bf16[4,2,128,128]{3,2,1,0:T(8,128)(2,1)} %copy-done.6, bf16[4,2,128,128]{3,2,1,0:T(8,128)(2,1)} %copy-done.5), custom_call_target="tpu_custom_call" | custom-call | flops 4294967296 | bytes 8388608 | tf_op jit(solution)/shard_map/attend_first/pallas_call | solution.py:365
  22.8 0.1 pad_maximum_fusion.3
  22.9 0.1 pad_maximum_fusion.2
  23.0 1.3 %collective-permute-start.5 = (bf16[8,2,128,128]{3,2,1,0:T(8,128)(2,1)S(1)}, bf16[8,2,128,128]{3,2,1,0:T(8,128)(2,1)S(1)}, u32[]{:S(2)}, u32[]{:S(2)}) collective-permute-start(bf16[8,2,128,128]{3,2,1,0:T(8,128)(2,1)S(1)} %pad_maximum_fusion.2), channel_id=1, source_target_pairs={{0,32},{1,5},{4,36},{5,1},{8,40},{9,13},{12,44},{13,9},{32,0},{33,... | collective-permute-start | bytes 1572872 | tf_op jit(solution)/shard_map/ppermute | solution.py:348
  24.2 1.8 %collective-permute-start.6 = (bf16[8,2,128,128]{3,2,1,0:T(8,128)(2,1)S(1)}, bf16[8,2,128,128]{3,2,1,0:T(8,128)(2,1)S(1)}, u32[]{:S(2)}, u32[]{:S(2)}) collective-permute-start(bf16[8,2,128,128]{3,2,1,0:T(8,128)(2,1)S(1)} %pad_maximum_fusion.3), channel_id=1, source_target_pairs={{0,96},{1,13},{4,100},{5,9},{8,104},{9,5},{12,108},{13,1},{32,64},... | collective-permute-start | bytes 1572872 | tf_op jit(solution)/shard_map/ppermute | solution.py:348
  26.1 9.1 %attend_second.1.refs_3_ = f32[2,2048,256]{2,1,0:T(8,128)} custom-call(s32[66]{0:T(128)} %pad_add_fusion.table.refs_0_, bf16[256,2048]{1,0:T(8,128)(2,1)} %q_ref.3, f32[2,2048,128]{2,1,0:T(8,128)} %get-tuple-element.13.refs_2_.top_in, f32[2,2048,256]{2,1,0:T(8,128)} %get-tuple-element.17.refs_3_, bf16[4,2,128,128]{3,2,1,0:T(8,128)(2,1)} %copy-done.8, ...), custom_call_target="tpu_custom_call" | custom-call | flops 4294967296 | bytes 8388608 | tf_op jit(solution)/shard_map/attend_second/pallas_call | solution.py:329
  35.2 0.1 pad_maximum_fusion.sa
  35.4 0.1 pad_maximum_fusion.1.sb
  35.5 0.9 %collective-permute-start.7 = (bf16[16,2,128,128]{3,2,1,0:T(8,128)(2,1)S(1)}, bf16[16,2,128,128]{3,2,1,0:T(8,128)(2,1)S(1)}, u32[]{:S(2)}, u32[]{:S(2)}) collective-permute-start(bf16[16,2,128,128]{3,2,1,0:T(8,128)(2,1)S(1)} %pad_maximum_fusion.sa), channel_id=1, source_target_pairs={{0,96},{1,13},{4,100},{5,9},{8,104},{9,5},{12,108},{13,1},{32,64},... | collective-permute-start | bytes 3145736 | tf_op jit(solution)/shard_map/ppermute | solution.py:348
  36.4 13.6 %attend_third.1.acc_in = f32[2,2048,256]{2,1,0:T(8,128)} custom-call(s32[66]{0:T(128)} %pad_add_fusion.table.refs_0_, bf16[256,2048]{1,0:T(8,128)(2,1)} %q_ref.3, f32[2,2048,128]{2,1,0:T(8,128)} %get-tuple-element.13.refs_2_.top_in, f32[2,2048,256]{2,1,0:T(8,128)} %attend_second.1.refs_3_, bf16[8,2,128,128]{3,2,1,0:T(8,128)(2,1)} %copy-done.3, ...), custom_call_target="tpu_custom_call" | custom-call | flops 8589934592 | bytes 8388608 | tf_op jit(solution)/shard_map/attend_third/pallas_call | solution.py:329
  50.1 0.6 collective-permute-done.7.a_ref.ra
  50.7 1.0 %copy-done.2 = bf16[16,2,128,128]{3,2,1,0:T(8,128)(2,1)} copy-done((bf16[16,2,128,128]{3,2,1,0:T(8,128)(2,1)}, bf16[16,2,128,128]{3,2,1,0:T(8,128)(2,1)S(1)}, u32[]{:S(2)}) %copy-start.2) | copy-done | bytes 1048600
  51.7 2.2 %pick_pages.1.mine = bf16[2,2,128,128]{3,2,1,0:T(8,128)(2,1)} custom-call(s32[66]{0:T(128)} %pad_add_fusion.table.refs_0_, bf16[16,2,128,128]{3,2,1,0:T(8,128)(2,1)} %copy-done, bf16[16,2,128,128]{3,2,1,0:T(8,128)(2,1)} %copy-done.2, bf16[16,2,128,128]{3,2,1,0:T(8,128)(2,1)} %copy-done.1, bf16[16,2,128,128]{3,2,1,0:T(8,128)(2,1)} %collective-permute-done.8.b_ref.rb), custom_call_target="tpu_custom_call" | custom-call | tf_op jit(solution)/shard_map/pick_pages/pallas_call | solution.py:383
  53.9 7.5 %collective-permute-start.11 = (bf16[2,2,128,128]{3,2,1,0:T(8,128)(2,1)}, bf16[2,2,128,128]{3,2,1,0:T(8,128)(2,1)S(1)}, u32[]{:S(2)}, u32[]{:S(2)}) collective-permute-start(bf16[2,2,128,128]{3,2,1,0:T(8,128)(2,1)} %pick_pages.1.mine), channel_id=1, source_target_pairs={{0,3},{1,2},{2,1},{3,0},{4,7},{5,6},{6,5},{7,4},{8,11},{9,10},{10,... | collective-permute-start | bytes 393224 | tf_op jit(solution)/shard_map/ppermute | solution.py:392
  61.4 0.5 collective-permute-start.9
  61.9 22.9 %attend_last.1 = bf16[256,2048]{1,0:T(8,128)(2,1)} custom-call(s32[66]{0:T(128)} %pad_add_fusion.table.refs_0_, bf16[256,2048]{1,0:T(8,128)(2,1)} %q_ref.3, f32[2,2048,128]{2,1,0:T(8,128)} %get-tuple-element.13.refs_2_.top_in, f32[2,2048,256]{2,1,0:T(8,128)} %attend_third.1.acc_in, bf16[16,2,128,128]{3,2,1,0:T(8,128)(2,1)} %copy-done.2, ...), custom_call_target="tpu_custom_call" | custom-call | flops 17179869184 | bytes 8388608 | tf_op jit(solution)/shard_map/attend_last/pallas_call | solution.py:394
  84.8 0.6 copy-done.9
  85.4 0.1 copy-done.10
  85.5 0.7 copy-done.11
  86.1 2.1 %place_pages.1 = (bf16[2,4,2,128,128]{4,3,2,1,0:T(8,128)(2,1)}, f32[2,2,4]{2,1,0:T(2,128)}) custom-call(bf16[2,2,128,128]{3,2,1,0:T(8,128)(2,1)} %pick_pages.1.mine, bf16[2,2,128,128]{3,2,1,0:T(8,128)(2,1)} %copy-done.11, bf16[2,2,128,128]{3,2,1,0:T(8,128)(2,1)} %copy-done.10, bf16[2,2,128,128]{3,2,1,0:T(8,128)(2,1)} %copy-done.9), custom_call_target="tpu_custom_call" | custom-call | tf_op jit(solution)/shard_map/place_pages/pallas_call | solution.py:413
  (35 shorter events, 0.2 us)
Async XLA Ops:
  1.5 5.7 %collective-permute-start = (bf16[2,1,2,128,128]{4,3,2,1,0:T(8,128)(2,1)S(1)}, bf16[2,1,2,128,128]{4,3,2,1,0:T(8,128)(2,1)S(1)}, u32[]{:S(2)}, u32[]{:S(2)}) collective-permute-start(bf16[2,1,2,128,128]{4,3,2,1,0:T(8,128)(2,1)S(1)} %maximum_bitcast_fusion), channel_id=1, source_target_pairs={{0,16},{16,0},{1,17},{17,1},{2,18},{18,2},{3,19},{19,3},{4,20},{20... | collective-permute-start | bytes 393224 | tf_op jit(solution)/shard_map/ppermute | solution.py:353
  7.3 5.1 %collective-permute-start.2 = (bf16[2,2,128,128]{3,2,1,0:T(8,128)(2,1)S(1)}, bf16[2,2,128,128]{3,2,1,0:T(8,128)(2,1)S(1)}, u32[]{:S(2)}, u32[]{:S(2)}) collective-permute-start(bf16[2,2,128,128]{3,2,1,0:T(8,128)(2,1)S(1)} %get-tuple-element.25), channel_id=1, source_target_pairs={{0,12},{1,97},{4,8},{5,101},{8,4},{9,105},{12,0},{13,109},{32,44},... | collective-permute-start | bytes 393224 | tf_op jit(solution)/shard_map/ppermute | solution.py:348
  10.2 4.2 %collective-permute-start.1 = (bf16[2,2,128,128]{3,2,1,0:T(8,128)(2,1)S(1)}, bf16[2,2,128,128]{3,2,1,0:T(8,128)(2,1)S(1)}, u32[]{:S(2)}, u32[]{:S(2)}) collective-permute-start(bf16[2,2,128,128]{3,2,1,0:T(8,128)(2,1)S(1)} %get-tuple-element.26), channel_id=1, source_target_pairs={{0,4},{1,33},{4,0},{5,37},{8,12},{9,41},{12,8},{13,45},{32,36},{33... | collective-permute-start | bytes 393224 | tf_op jit(solution)/shard_map/ppermute | solution.py:348
  12.4 2.9 %copy-start.5 = (bf16[4,2,128,128]{3,2,1,0:T(8,128)(2,1)}, bf16[4,2,128,128]{3,2,1,0:T(8,128)(2,1)S(1)}, u32[]{:S(2)}) copy-start(bf16[4,2,128,128]{3,2,1,0:T(8,128)(2,1)S(1)} %pad_maximum_fusion.5.b_ref) | copy-start | bytes 786436
  12.4 10.3 %collective-permute-start.4 = (bf16[4,2,128,128]{3,2,1,0:T(8,128)(2,1)S(1)}, bf16[4,2,128,128]{3,2,1,0:T(8,128)(2,1)S(1)}, u32[]{:S(2)}, u32[]{:S(2)}) collective-permute-start(bf16[4,2,128,128]{3,2,1,0:T(8,128)(2,1)S(1)} %pad_maximum_fusion.5.b_ref), channel_id=1, source_target_pairs={{0,4},{1,33},{4,0},{5,37},{8,12},{9,41},{12,8},{13,45},{32,36},{33... | collective-permute-start | bytes 786440 | tf_op jit(solution)/shard_map/ppermute | solution.py:348
  14.4 0.9 %copy-start.6 = (bf16[4,2,128,128]{3,2,1,0:T(8,128)(2,1)}, bf16[4,2,128,128]{3,2,1,0:T(8,128)(2,1)S(1)}, u32[]{:S(2)}) copy-start(bf16[4,2,128,128]{3,2,1,0:T(8,128)(2,1)S(1)} %pad_maximum_fusion.4.a_ref) | copy-start | bytes 786436
  14.4 8.4 %collective-permute-start.3 = (bf16[4,2,128,128]{3,2,1,0:T(8,128)(2,1)S(1)}, bf16[4,2,128,128]{3,2,1,0:T(8,128)(2,1)S(1)}, u32[]{:S(2)}, u32[]{:S(2)}) collective-permute-start(bf16[4,2,128,128]{3,2,1,0:T(8,128)(2,1)S(1)} %pad_maximum_fusion.4.a_ref), channel_id=1, source_target_pairs={{0,12},{1,97},{4,8},{5,101},{8,4},{9,105},{12,0},{13,109},{32,44},... | collective-permute-start | bytes 786440 | tf_op jit(solution)/shard_map/ppermute | solution.py:348
  22.8 3.3 %copy-start.7 = (bf16[4,2,128,128]{3,2,1,0:T(8,128)(2,1)}, bf16[4,2,128,128]{3,2,1,0:T(8,128)(2,1)S(1)}, u32[]{:S(2)}) copy-start(bf16[4,2,128,128]{3,2,1,0:T(8,128)(2,1)S(1)} %collective-permute-done.4.refs_5_) | copy-start | bytes 786436
  22.9 3.2 %copy-start.8 = (bf16[4,2,128,128]{3,2,1,0:T(8,128)(2,1)}, bf16[4,2,128,128]{3,2,1,0:T(8,128)(2,1)S(1)}, u32[]{:S(2)}) copy-start(bf16[4,2,128,128]{3,2,1,0:T(8,128)(2,1)S(1)} %collective-permute-done.3.refs_4_) | copy-start | bytes 786436
  23.0 12.2 %collective-permute-start.5 = (bf16[8,2,128,128]{3,2,1,0:T(8,128)(2,1)S(1)}, bf16[8,2,128,128]{3,2,1,0:T(8,128)(2,1)S(1)}, u32[]{:S(2)}, u32[]{:S(2)}) collective-permute-start(bf16[8,2,128,128]{3,2,1,0:T(8,128)(2,1)S(1)} %pad_maximum_fusion.2), channel_id=1, source_target_pairs={{0,32},{1,5},{4,36},{5,1},{8,40},{9,13},{12,44},{13,9},{32,0},{33,... | collective-permute-start | bytes 1572872 | tf_op jit(solution)/shard_map/ppermute | solution.py:348
  24.2 11.1 %collective-permute-start.6 = (bf16[8,2,128,128]{3,2,1,0:T(8,128)(2,1)S(1)}, bf16[8,2,128,128]{3,2,1,0:T(8,128)(2,1)S(1)}, u32[]{:S(2)}, u32[]{:S(2)}) collective-permute-start(bf16[8,2,128,128]{3,2,1,0:T(8,128)(2,1)S(1)} %pad_maximum_fusion.3), channel_id=1, source_target_pairs={{0,96},{1,13},{4,100},{5,9},{8,104},{9,5},{12,108},{13,1},{32,64},... | collective-permute-start | bytes 1572872 | tf_op jit(solution)/shard_map/ppermute | solution.py:348
  35.2 1.2 %copy-start.3 = (bf16[8,2,128,128]{3,2,1,0:T(8,128)(2,1)}, bf16[8,2,128,128]{3,2,1,0:T(8,128)(2,1)S(1)}, u32[]{:S(2)}) copy-start(bf16[8,2,128,128]{3,2,1,0:T(8,128)(2,1)S(1)} %collective-permute-done.5.refs_4_) | copy-start | bytes 1572868
  35.3 14.7 %copy-start = (bf16[16,2,128,128]{3,2,1,0:T(8,128)(2,1)}, bf16[16,2,128,128]{3,2,1,0:T(8,128)(2,1)S(1)}, u32[]{:S(2)}) copy-start(bf16[16,2,128,128]{3,2,1,0:T(8,128)(2,1)S(1)} %pad_maximum_fusion.sa) | copy-start | bytes 3145732
  35.3 1.1 %copy-start.4 = (bf16[8,2,128,128]{3,2,1,0:T(8,128)(2,1)}, bf16[8,2,128,128]{3,2,1,0:T(8,128)(2,1)S(1)}, u32[]{:S(2)}) copy-start(bf16[8,2,128,128]{3,2,1,0:T(8,128)(2,1)S(1)} %collective-permute-done.6.refs_5_) | copy-start | bytes 1572868
  35.5 14.6 %copy-start.1 = (bf16[16,2,128,128]{3,2,1,0:T(8,128)(2,1)}, bf16[16,2,128,128]{3,2,1,0:T(8,128)(2,1)S(1)}, u32[]{:S(2)}) copy-start(bf16[16,2,128,128]{3,2,1,0:T(8,128)(2,1)S(1)} %pad_maximum_fusion.1.sb) | copy-start | bytes 3145732
  35.5 15.2 %collective-permute-start.7 = (bf16[16,2,128,128]{3,2,1,0:T(8,128)(2,1)S(1)}, bf16[16,2,128,128]{3,2,1,0:T(8,128)(2,1)S(1)}, u32[]{:S(2)}, u32[]{:S(2)}) collective-permute-start(bf16[16,2,128,128]{3,2,1,0:T(8,128)(2,1)S(1)} %pad_maximum_fusion.sa), channel_id=1, source_target_pairs={{0,96},{1,13},{4,100},{5,9},{8,104},{9,5},{12,108},{13,1},{32,64},... | collective-permute-start | bytes 3145736 | tf_op jit(solution)/shard_map/ppermute | solution.py:348
  36.4 14.3 %collective-permute-start.8 = (bf16[16,2,128,128]{3,2,1,0:T(8,128)(2,1)S(1)}, bf16[16,2,128,128]{3,2,1,0:T(8,128)(2,1)}, u32[]{:S(2)}, u32[]{:S(2)}) collective-permute-start(bf16[16,2,128,128]{3,2,1,0:T(8,128)(2,1)S(1)} %pad_maximum_fusion.1.sb), channel_id=1, source_target_pairs={{0,32},{1,5},{4,36},{5,1},{8,40},{9,13},{12,44},{13,9},{32,0},{33,... | collective-permute-start | bytes 3145736 | tf_op jit(solution)/shard_map/ppermute | solution.py:348
  50.7 1.0 %copy-start.2 = (bf16[16,2,128,128]{3,2,1,0:T(8,128)(2,1)}, bf16[16,2,128,128]{3,2,1,0:T(8,128)(2,1)S(1)}, u32[]{:S(2)}) copy-start(bf16[16,2,128,128]{3,2,1,0:T(8,128)(2,1)S(1)} %collective-permute-done.7.a_ref.ra) | copy-start | bytes 3145732
  53.9 30.9 %collective-permute-start.11 = (bf16[2,2,128,128]{3,2,1,0:T(8,128)(2,1)}, bf16[2,2,128,128]{3,2,1,0:T(8,128)(2,1)S(1)}, u32[]{:S(2)}, u32[]{:S(2)}) collective-permute-start(bf16[2,2,128,128]{3,2,1,0:T(8,128)(2,1)} %pick_pages.1.mine), channel_id=1, source_target_pairs={{0,3},{1,2},{2,1},{3,0},{4,7},{5,6},{6,5},{7,4},{8,11},{9,10},{10,... | collective-permute-start | bytes 393224 | tf_op jit(solution)/shard_map/ppermute | solution.py:392
  61.4 23.4 %collective-permute-start.10 = (bf16[2,2,128,128]{3,2,1,0:T(8,128)(2,1)}, bf16[2,2,128,128]{3,2,1,0:T(8,128)(2,1)S(1)}, u32[]{:S(2)}, u32[]{:S(2)}) collective-permute-start(bf16[2,2,128,128]{3,2,1,0:T(8,128)(2,1)} %pick_pages.1.mine), channel_id=1, source_target_pairs={{0,2},{1,3},{2,0},{3,1},{4,6},{5,7},{6,4},{7,5},{8,10},{9,11},{10,... | collective-permute-start | bytes 393224 | tf_op jit(solution)/shard_map/ppermute | solution.py:392
  61.4 23.4 %collective-permute-start.9 = (bf16[2,2,128,128]{3,2,1,0:T(8,128)(2,1)}, bf16[2,2,128,128]{3,2,1,0:T(8,128)(2,1)S(1)}, u32[]{:S(2)}, u32[]{:S(2)}) collective-permute-start(bf16[2,2,128,128]{3,2,1,0:T(8,128)(2,1)} %pick_pages.1.mine), channel_id=1, source_target_pairs={{0,1},{1,0},{2,3},{3,2},{4,5},{5,4},{6,7},{7,6},{8,9},{9,8},{10,11... | collective-permute-start | bytes 393224 | tf_op jit(solution)/shard_map/ppermute | solution.py:392
  84.8 0.6 copy-start.9
  84.8 0.7 copy-start.10
  85.5 0.7 copy-start.11
